TPU v7x, 32 devices: a whole 2x2x4 slice. The times are simulated.
32 devices in a mesh: stream: 16 (over z, y, x), cross: 2 (over core).
Axes of the slice: x: 2, y: 2, z: 4, core: 2. Of those that a mesh axis runs over, the one named last changes fastest.
Arguments:
- source: float32 [128, 16, 128], P('stream', 'cross'), may hold values from -6 to 6
- metric: float32 [16, 2, 16], P('stream', 'cross'), may hold values from 0.5 to 4
- base_velocity: float32 [3, 128, 16, 128], P(None, 'stream', 'cross'), may hold values from -6 to 6
- drop_elem: int32 [16, 2, 5, 128], P('stream', 'cross'), may hold values from 0 to 511, as said below
- drop_coord: float32 [16, 2, 5, 3, 128], P('stream', 'cross'), may hold values from -1 to 1
- drop_vel: float32 [16, 2, 5, 3, 128], P('stream', 'cross'), may hold values from -6 to 6
- drop_prop: float32 [16, 2, 5, 2, 128], P('stream', 'cross'), may hold values from 0.5 to 4
- drop_counts: int32 [16, 2, 5], P('stream', 'cross'), may hold values from 0 to 128, as said below
Outputs:
- pressure: float32 [128, 16, 128], P('stream', 'cross')
- momentum_source: float32 [3, 128, 16, 128], P(None, 'stream', 'cross')
- drop_accel: float32 [16, 2, 5, 3, 128], P('stream', 'cross')
Inputs may be any that keep to these rules, and one draw needn't show every extreme that they name: `drop_elem`: elements are numbered (ex * 2 + ey) * 16 + ez. The owner element of every slot of block b of holder (s, c) lies in slab s + b - 2 (streamwise element index from (s + b - 2) * 1 to that plus 1 - 1) and column c (element index from c * 1 to c + 1 - 1); this holds for slots that are not live as well, for blocks whose slab lies in the grid. `drop_counts`: A block whose owner slab s + b - 2 lies outside 0 to 15 has count 0. In every draw some slab of some column receives 128 live droplets from each of its 5 holder slabs.
All inputs are finite; a program needn't handle non-finite values.
Results may differ from a plain program's by a relative error of at most 0.0003.
Values sent between devices are 32-bit elements; how exact they have to be, the bound alone decides.
No kernel may reach another device: no remote copies, remote signals or barrier semaphores. Data moves between devices by JAX's collectives and lax.ppermute only.
A program may use at most 64 MiB of HBM per device.

v0:
```python
import jax
import jax.numpy as jnp
import numpy as np
from jax import lax
from jax.experimental import pallas as pl
from jax.experimental.pallas import tpu as pltpu
from jax.sharding import PartitionSpec as P


SWEEPS = 3
DEPTH = SWEEPS + 1
NODES = 8
MASS_SHIFT = 1.0
UPPER_BOUND = 2.5
LOWER_BOUND = UPPER_BOUND / 30.0
GLL_POINTS = [
    -1.0,
    -0.8717401485096066,
    -0.5917001814331423,
    -0.2092992179024789,
    0.2092992179024789,
    0.5917001814331423,
    0.8717401485096066,
    1.0,
]
F32 = jnp.float32
BF16 = jnp.bfloat16


def legendre_seven(points):
    before = points * 0.0 + 1.0
    current = points
    for order in range(1, 7):
        following = ((2.0 * order + 1.0) * points * current - order * before) / (order + 1.0)
        before = current
        current = following
    return current


def gll_tables():
    gll_nodes = np.array(GLL_POINTS)
    values = legendre_seven(gll_nodes)
    weights = 2.0 / (56.0 * values * values)
    deriv_mat = np.zeros((8, 8))
    for row_idx in range(8):
        for col_idx in range(8):
            if row_idx != col_idx:
                deriv_mat[row_idx, col_idx] = values[row_idx] / (
                    values[col_idx] * (gll_nodes[row_idx] - gll_nodes[col_idx])
                )
    deriv_mat[0, 0] = -14.0
    deriv_mat[7, 7] = 14.0
    return (gll_nodes, weights, deriv_mat)


NODE_POS, WEIGHTS, DERIV = gll_tables()
STIFF = DERIV.T @ (WEIGHTS[:, None] * DERIV)
STIFF_DIAG = np.diag(STIFF)


def split_pair(table):
    high = table.astype(np.float32).astype(jnp.bfloat16)
    low = (table - high.astype(np.float64)).astype(np.float32).astype(jnp.bfloat16)
    return high, low


def lane_weights(matrix, lanes, summed):
    full = np.kron(np.eye(lanes // NODES), matrix.T)
    if summed:
        shared = np.eye(lanes)
        for last in range(NODES - 1, lanes - 1, NODES):
            shared[last, last + 1] = shared[last + 1, last] = 1.0
        full = full @ shared
    high, low = split_pair(full)
    zero = np.zeros_like(np.asarray(low))
    return np.concatenate(
        [np.concatenate([high, low], 1), np.concatenate([high, zero], 1)], 0
    ).astype(jnp.bfloat16)


F_FACE = (DEPTH - 1) * NODES
F_META = F_FACE + 1
F_COUNT = F_FACE + 2
ROUTES = ((1, 0), (1, 1), (2, 0), (2, 1))
T_KY, T_DY = 0, 8
T_WJ, T_QJ, T_WK, T_QK, T_Z7, T_Z0, T_Y7, T_Y0 = range(16, 24)
T_NODE = 24
T_INV = 31
T_WKS = 32
T_COUNT = 33
HALF = NODES // 2


def table_tiles(lanes):
    tiles = np.zeros((T_COUNT, NODES, lanes))
    for turn in range(NODES):
        outer, inner = turn % HALF, turn - turn % HALF
        for row in range(NODES):
            to, of = (row + outer) % NODES, (row - inner) % NODES
            tiles[T_KY + turn, row, :] = STIFF[to, of]
            tiles[T_DY + turn, row, :] = DERIV[to, of]
    reps = lanes // NODES
    tiles[T_WJ] = WEIGHTS[:, None]
    tiles[T_QJ] = STIFF_DIAG[:, None]
    tiles[T_WK] = np.tile(WEIGHTS, reps)[None, :]
    tiles[T_QK] = np.tile(STIFF_DIAG, reps)[None, :]
    place = np.arange(lanes)
    tiles[T_Z7] = ((place % NODES == NODES - 1) & (place < lanes - 1))[None, :]
    tiles[T_Z0] = ((place % NODES == 0) & (place > 0))[None, :]
    assembled = np.tile(WEIGHTS, reps)
    assembled[NODES - 1 : -1 : NODES] += WEIGHTS[0]
    assembled[NODES::NODES] += WEIGHTS[-1]
    tiles[T_WKS] = assembled[None, :]
    tiles[T_Y7, NODES - 1] = 1.0
    tiles[T_Y0, 0] = 1.0
    for row in range(NODES):
        others = [m for m in range(NODES) if m != row]
        scale = 1.0
        for slot, other in enumerate(others):
            tiles[T_NODE + slot, row, :] = NODE_POS[other]
            scale *= NODE_POS[row] - NODE_POS[other]
        tiles[T_INV, row, :] = 1.0 / scale
    return tiles.astype(np.float32)


def swapped_bit(slabs, cols, bit):
    return [
        (i * cols + j, (i ^ bit) * cols + (j ^ 1)) for i in range(slabs) for j in range(cols)
    ]


def neighbours(slabs, cols, distance, odd, swap=0):
    partner = {}
    for low in range(slabs - distance):
        if (low // distance) % 2 == odd:
            partner[low] = low + distance
            partner[low + distance] = low
    pairs = []
    for i in range(slabs):
        for j in range(cols):
            if i in partner:
                pairs.append((i * cols + j, partner[i] * cols + (j ^ swap)))
            else:
                pairs.append((i * cols + j, i * cols + (j ^ 1)))
    return pairs


def column_pairs(cols, bit):
    return [(j, j ^ bit) for j in range(cols)]


def side_pairs(cols, odd):
    pairs = []
    for low in range(cols - 1):
        if low % 2 == odd:
            pairs += [(low, low + 1), (low + 1, low)]
    return pairs


def parity(slot):
    return bin(slot).count("1") % 2


def route_partner(position, route):
    distance, odd = route
    upward = (position // distance) % 2 == odd
    return jnp.where(upward, position + distance, position - distance), upward


def route_block(position, route, reach):
    middle = (reach - 1) // 2
    upward = route_partner(position, route)[1]
    return jnp.where(upward, middle + route[0], middle - route[0])


def route_open(position, route, slabs):
    partner = route_partner(position, route)[0]
    return jnp.logical_and(partner >= 0, partner < slabs)


def split_value(value):
    high = value.astype(BF16)
    low = (value - high.astype(F32)).astype(BF16)
    return high, low


def pack_kernel(cols, elem_z, source, metric, elem, coord, vel, prop, counts, first, own, *rest):
    first[0:NODES] = source[...]
    first[NODES] = jnp.zeros(first.shape[1:], F32)
    first[NODES, 0:1, 0 : metric.shape[-1]] = metric[0]
    routed, state = rest[:-1], rest[-1]
    position = lax.axis_index("stream")
    column = lax.axis_index("cross")
    reach, _, capacity = elem.shape
    middle = (reach - 1) // 2
    slot = lax.broadcasted_iota(jnp.int32, (1, capacity), 1)
    for block in range(reach):
        base = ((position + (block - middle)) * cols + column) * elem_z
        live = slot < counts[0, 0, block]
        ids = jnp.where(live, elem[block] - base + 1, 0).astype(F32)
        for axis in range(3):
            state[block, 0, axis : axis + 1, :] = coord[3 * block + axis]
            state[block, 0, 3 + axis : 4 + axis, :] = vel[3 * block + axis]
        state[block, 0, 6:8, :] = prop[0, 0, block]
        state[block, 1] = jnp.broadcast_to(ids, (NODES, capacity))
    own[...] = state[middle]
    for route, out in zip(ROUTES, routed):
        out[...] = state[route_block(position, route, reach)]


def near_kernel(first, from_source, from_metric, out):
    out[0] = first[...]
    out[1, 0:NODES] = from_source[...]
    out[1, NODES] = jnp.zeros(out.shape[2:], F32)
    out[1, NODES, 0:1, 0 : from_metric.shape[-1]] = from_metric[0]


def far_kernel(gathered, *outs):
    position = lax.axis_index("stream")
    group_even = (position // DEPTH) % 2 == 0
    for odd, out in enumerate(outs):
        upward = group_even if odd == 0 else jnp.logical_not(group_even)
        for slot in range(1, DEPTH):
            for i in range(NODES):
                out[(slot - 1) * NODES + i] = gathered[slot, i]
        out[F_FACE] = gathered[0, jnp.where(upward, NODES - 1, 0)]
        out[F_META] = jnp.zeros(out.shape[1:], F32)
        for slot in range(DEPTH):
            out[F_META, slot : slot + 1, :] = gathered[slot, NODES, 0:1, :]


def z_assembled(block, tiles):
    lanes = block.shape[-1]
    axis = block.ndim - 1
    after = pltpu.roll(block, lanes - 1, axis)
    before = pltpu.roll(block, 1, axis)
    return block + tiles[T_Z7] * after + tiles[T_Z0] * before


def y_assembled(blocks, tiles):
    axis = blocks[0].ndim - 2
    out = []
    for j, block in enumerate(blocks):
        total = block
        if j + 1 < len(blocks):
            total = total + tiles[T_Y7] * pltpu.roll(blocks[j + 1], NODES - 1, axis)
        if j > 0:
            total = total + tiles[T_Y0] * pltpu.roll(blocks[j - 1], 1, axis)
        out.append(total)
    return out


def halves(planes):
    even = [planes[m] + planes[NODES - 1 - m] for m in range(HALF)]
    odd = [planes[m] - planes[NODES - 1 - m] for m in range(HALF)]
    return even, odd


def row_pair(even, odd, matrix, row, mirrored):
    sums = []
    for values, sign in ((even, 0.5), (odd, -0.5)):
        total = None
        for m in range(HALF):
            factor = 0.5 * matrix[row, m] + sign * matrix[row, NODES - 1 - m]
            term = values[m] * float(factor)
            total = term if total is None else total + term
        sums.append(total)
    first = sums[0] + sums[1]
    second = sums[0] - sums[1] if mirrored > 0 else sums[1] - sums[0]
    return first, second


def x_product(planes, matrix, mirrored):
    even, odd = halves(planes)
    pairs = [row_pair(even, odd, matrix, row, mirrored) for row in range(HALF)]
    return [pair[0] for pair in pairs] + [pair[1] for pair in reversed(pairs)]


def y_product(block, tiles, start):
    axis = block.ndim - 2
    far = pltpu.roll(block, HALF, axis)
    total = None
    for outer in range(HALF):
        part = block * tiles[start + outer] + far * tiles[start + HALF + outer]
        if outer > 0:
            part = pltpu.roll(part, outer, axis)
        total = part if total is None else total + part
    return total


def z_product(rows, weights):
    lanes = rows.shape[-1]
    high, low = split_value(rows)
    both = jnp.concatenate([high, low], axis=1)
    wide = jnp.dot(both, weights, preferred_element_type=F32)
    return wide[:, :lanes] + wide[:, lanes:]


def lagrange(row, tiles):
    capacity = row.shape[-1]
    coords = jnp.broadcast_to(row, (NODES, capacity))
    factor = tiles[T_INV]
    for slot in range(NODES - 1):
        factor = factor * (coords - tiles[T_NODE + slot])
    return factor


def main_kernel(slabs, cols, *refs):
    tiles, stiff_w, deriv_w, spread_w = refs[0:4]
    pieces = refs[4 : 4 + 3 * cols]
    base_velocity, own = refs[4 + 3 * cols : 6 + 3 * cols]
    routed = refs[6 + 3 * cols : 10 + 3 * cols]
    (pressure, momentum, face_even, face_odd, acc_own, acc_e1, acc_o1, acc_e2, acc_o2,
     loads, scales, resid, update, inv, work, spans, layers) = refs[10 + 3 * cols :]
    lanes = tiles.shape[-1]
    position = lax.axis_index("stream")
    column = lax.axis_index("cross")
    middle = DEPTH - 1

    group_even = (position // DEPTH) % 2 == 0
    rank = position % DEPTH
    wjk = tiles[T_WJ] * tiles[T_WK]
    flat = (NODES, lanes)

    def present(offset):
        where = position + offset
        return jnp.where((where >= 0) & (where < slabs), 1.0, 0.0).astype(F32)

    factors = []
    for slot_c in range(cols):
        near, *fars = pieces[3 * slot_c : 3 * slot_c + 3]
        factors += [near[slot, NODES, 0:1, :] for slot in range(DEPTH)]
        factors += [jnp.zeros((NODES - DEPTH, lanes), F32)] + [far[F_META] for far in fars]
    high, low = split_value(jnp.concatenate(factors, 0))
    factors = jnp.dot(
        jnp.concatenate([high, low], 1), spread_w[...], preferred_element_type=F32
    )
    for slot_c in range(cols):
        near, *fars = pieces[3 * slot_c : 3 * slot_c + 3]
        for slot in range(DEPTH):
            col = column ^ (slot_c ^ parity(slot))
            at = (rank ^ slot) - rank + (2 * DEPTH - 1)
            for i in range(NODES):
                loads[at, col, i] = near[slot, i] * (wjk * float(WEIGHTS[i]))
            row = 3 * NODES * slot_c + slot
            scales[at, col] = jnp.broadcast_to(factors[row : row + 1], flat)
        for odd, far in enumerate(fars):
            upper = group_even if odd == 0 else jnp.logical_not(group_even)
            shift = jnp.where(upper, DEPTH, -DEPTH)
            inside = present(shift)
            for slot in range(DEPTH):
                col = column ^ (slot_c ^ parity(slot) ^ 1)
                at = (rank ^ slot) - rank + shift + (2 * DEPTH - 1)
                if slot > 0:
                    for i in range(NODES):
                        loads[at, col, i] = far[(slot - 1) * NODES + i] * (
                            wjk * (inside * float(WEIGHTS[i]))
                        )
                else:
                    layer = jnp.where(upper, 0, NODES - 1)
                    loads[at, col, layer] = far[F_FACE] * (wjk * (inside * float(WEIGHTS[0])))
                row = 3 * NODES * slot_c + NODES * (1 + odd) + slot
                scales[at, col] = jnp.broadcast_to(factors[row : row + 1] * inside, flat)
    wide_mid = 2 * DEPTH - 1

    columns = range(cols)
    for offset in range(-DEPTH, DEPTH + 1):
        at = wide_mid + offset
        mass = (MASS_SHIFT * present(offset)) * tiles[T_WKS]
        alphas = [z_assembled(scales[at, j] * tiles[T_WK], tiles) for j in columns]
        betas = [z_assembled(scales[at, j] * tiles[T_QK], tiles) + mass for j in columns]
        sigmas = y_assembled([tiles[T_WJ] * alphas[j] for j in columns], tiles)
        taus = y_assembled([tiles[T_WJ] * scales[at, j] for j in columns], tiles)
        rests = y_assembled(
            [tiles[T_QJ] * alphas[j] + tiles[T_WJ] * betas[j] for j in columns], tiles
        )
        masses = y_assembled([tiles[T_WJ] * mass] * cols, tiles)
        for j in columns:
            for index, value in enumerate((alphas[j], sigmas[j], taus[j], rests[j], masses[j])):
                spans[index, DEPTH + offset, j] = value
        if abs(offset) < DEPTH:
            sides = [loads[at, j] for j in columns]
            sides = y_assembled([z_assembled(side, tiles) for side in sides], tiles)
            for j in columns:
                work[DEPTH + offset, j] = sides[j]
        else:
            layer = NODES - 1 if offset < 0 else 0
            sides = [loads[at, j, layer] for j in columns]
            sides = y_assembled([z_assembled(side, tiles) for side in sides], tiles)
            for j in columns:
                work[DEPTH + offset, j, layer] = sides[j]

    center = (UPPER_BOUND + LOWER_BOUND) / 2.0
    half_width = (UPPER_BOUND - LOWER_BOUND) / 2.0
    ratio_bound = center / half_width
    cheb_rho = 1.0 / ratio_bound
    ends = {0: -1, NODES - 1: 1}

    def joined(index, offset, j, i):
        tile = spans[index, DEPTH + offset, j]
        if i in ends:
            tile = tile + spans[index, DEPTH + offset + ends[i], j]
        return tile

    for offset in range(-middle, middle + 1):
        at = middle + offset
        gap = 1.0 - present(offset)
        for j in columns:
            for i in range(NODES):
                side = work[DEPTH + offset, j, i]
                if i in ends:
                    side = side + work[DEPTH + offset + ends[i], j, NODES - 1 - i]
                diag = joined(1, offset, j, i) * float(STIFF_DIAG[i]) + (
                    joined(3, offset, j, i) * float(WEIGHTS[i]) + gap
                )
                inverse = 1.0 / diag
                inv[at, j, i] = inverse
                resid[at, j, i] = side
                update[at, j, i] = side * inverse * (1.0 / center)

    iterate = update[middle, column]
    for sweep in range(SWEEPS):
        reach = SWEEPS - 1 - sweep
        rho_next = 1.0 / (2.0 * ratio_bound - cheb_rho)
        for offset in range(-reach - 1, reach + 2):
            for j in columns:
                sigma = spans[1, DEPTH + offset, j]
                planes = [sigma * update[middle + offset, j, i] for i in range(NODES)]
                first, last = row_pair(*halves(planes), STIFF, 0, 1)
                layers[DEPTH + offset, j, 0] = first
                layers[DEPTH + offset, j, 1] = last
        for offset in range(-reach, reach + 1):
            at = middle + offset
            weighted = [[update[at, j, i] * float(WEIGHTS[i]) for i in range(NODES)] for j in columns]
            rows = [
                joined(2, offset, j, i) * weighted[j][i] for j in columns for i in range(NODES)
            ]
            from_z = z_product(jnp.concatenate(rows, 0), stiff_w[...])
            from_y = y_assembled(
                [
                    y_product(
                        jnp.stack([joined(0, offset, j, i) * weighted[j][i] for i in range(NODES)], 0),
                        tiles,
                        T_KY,
                    )
                    for j in columns
                ],
                tiles,
            )
            for j in columns:
                sigma = spans[1, DEPTH + offset, j]
                planes = [sigma * update[at, j, i] for i in range(NODES)]
                even, odd = halves(planes)
                from_x = [None] * NODES
                from_x[0] = layers[DEPTH + offset, j, 0] + layers[DEPTH + offset - 1, j, 1]
                from_x[-1] = layers[DEPTH + offset, j, 1] + layers[DEPTH + offset + 1, j, 0]
                for row in range(1, HALF):
                    from_x[row], from_x[NODES - 1 - row] = row_pair(even, odd, STIFF, row, 1)
                for i in range(NODES):
                    row = (j * NODES + i) * NODES
                    total = from_x[i] + from_y[j][i] + from_z[row : row + NODES]
                    total = total + joined(4, offset, j, i) * weighted[j][i]
                    left = resid[at, j, i] - total
                    resid[at, j, i] = left
                    update[at, j, i] = (rho_next * cheb_rho) * update[at, j, i] + (
                        2.0 * rho_next / half_width
                    ) * (inv[at, j, i] * left)
        cheb_rho = rho_next
        iterate = iterate + update[middle, column]
    pressure[...] = iterate

    scale = scales[wide_mid, column]
    planes = [iterate[i] for i in range(NODES)]
    grad_x = x_product(planes, DERIV, -1)
    grad_z = z_product(iterate.reshape(NODES * NODES, lanes), deriv_w[...]).reshape(NODES, NODES, lanes)
    velocity = []
    for i in range(NODES):
        velocity.append(base_velocity[0, i] - scale * grad_x[i])
    for i in range(NODES):
        velocity.append(base_velocity[1, i] - scale * y_product(planes[i], tiles, T_DY))
    for i in range(NODES):
        velocity.append(base_velocity[2, i] - scale * grad_z[i])
    velocity = jnp.concatenate(velocity, 0)

    groups = [(own[0], own[1])]
    for route, group in zip(ROUTES, routed):
        groups.append((group[0], jnp.where(route_open(position, route, slabs), group[1], 0.0)))
    pick, bases = [], []
    for group, ids in groups:
        basis = [lagrange(group[axis : axis + 1, :], tiles) for axis in range(3)]
        pick.append(jnp.concatenate(
            [jnp.where(ids == float(e + 1), basis[2], 0.0) for e in range(lanes // NODES)], 0))
        bases.append(basis)
    pick = jnp.concatenate(pick, 1)
    pick_high, pick_low = split_value(pick)
    vel_high, vel_low = split_value(velocity)
    partial = jnp.dot(
        jnp.concatenate([vel_high, vel_low, vel_high], 1),
        jnp.concatenate([pick_high, pick_high, pick_low], 0),
        preferred_element_type=F32,
    )
    capacity = own.shape[-1]
    spread = []
    for g, ((group, ids), basis) in enumerate(zip(groups, bases)):
        cells = [basis[1] * basis[0][i : i + 1, :] for i in range(NODES)]
        accel_rows, parts = [], []
        for comp in range(3):
            total = None
            for i in range(NODES):
                row = (comp * NODES + i) * NODES
                term = partial[row : row + NODES, g * capacity : (g + 1) * capacity] * cells[i]
                total = term if total is None else total + term
            fluid = jnp.sum(total, axis=0, keepdims=True)
            accel = jnp.where(ids[0:1, :] > 0.5, group[6:7, :] * (fluid - group[3 + comp : 4 + comp, :]), 0.0)
            accel_rows.append(accel)
            force = -group[7:8, :] * accel
            parts += [cells[i] * force for i in range(NODES)]
        accel_rows.append(jnp.zeros((NODES - 3, capacity), F32))
        (acc_own, acc_e1, acc_o1, acc_e2, acc_o2)[g][...] = jnp.concatenate(accel_rows, 0)
        spread.append(jnp.concatenate(parts, 0))
    spread = jnp.concatenate(spread, 1)
    spread_high, spread_low = split_value(spread)
    added = lax.dot_general(
        jnp.concatenate([spread_high, spread_low, spread_high], 1),
        jnp.concatenate([pick_high, pick_high, pick_low], 1),
        (((1,), (1,)), ((), ())),
        preferred_element_type=F32,
    )
    added = z_assembled(added.reshape(3, NODES, NODES, lanes), tiles)
    momentum[...] = added
    low_row = added[:, :, 0, :]
    high_row = added[:, :, NODES - 1, :]
    even = column % 2 == 0
    face_even[...] = jnp.where(even, high_row, low_row)
    face_odd[...] = jnp.where(even, low_row, high_row)


def middle_kernel(cols, momentum, face_even, face_odd, acc_e1, acc_o1, out, send_e1, send_o1):
    position = lax.axis_index("stream")
    column = lax.axis_index("cross")
    even = column % 2 == 0
    high = jnp.where(even, face_even[...], face_odd[...]) if cols > 2 else jnp.where(even, face_even[...], 0.0)
    low = jnp.where(even, face_odd[...], face_even[...]) if cols > 2 else jnp.where(even, 0.0, face_even[...])
    out[...] = momentum[...]
    out[:, :, 0, :] = momentum[:, :, 0, :] + low
    out[:, :, NODES - 1, :] = momentum[:, :, NODES - 1, :] + high
    lower = position % 2 == 0
    top = jnp.where(lower, NODES - 1, 0)
    bottom = NODES - 1 - top
    for comp in range(3):
        send_e1[comp] = out[comp, top]
        send_o1[comp] = out[comp, bottom]
    send_e1[3] = acc_e1[...]
    send_o1[3] = acc_o1[...]


def last_kernel(slabs, reach, momentum, got_e1, got_o1, acc_own, got_e2, got_o2, out, accel):
    position = lax.axis_index("stream")
    lower = position % 2 == 0
    top = jnp.where(lower, NODES - 1, 0)
    bottom = NODES - 1 - top
    out[...] = momentum[...]
    opened = [route_open(position, route, slabs) for route in ROUTES]
    for comp in range(3):
        out[comp, top] = momentum[comp, top] + jnp.where(opened[0], got_e1[comp], 0.0)
        out[comp, bottom] = momentum[comp, bottom] + jnp.where(opened[1], got_o1[comp], 0.0)
    for axis in range(3):
        accel[3 * ((reach - 1) // 2) + axis] = acc_own[axis : axis + 1]
    arrived = (got_e1[3], got_o1[3], got_e2[...], got_o2[...])
    for route, value, there in zip(ROUTES, arrived, opened):
        block = route_block(position, route, reach)
        for axis in range(3):
            accel[3 * block + axis] = jnp.where(there, value[axis : axis + 1], 0.0)


def f32(*shape):
    return jax.ShapeDtypeStruct(shape, F32)


def near(*shape):
    return pltpu.VMEM(shape, F32)


def held(value):
    return pltpu.with_memory_space_constraint(value, pltpu.VMEM)


def step(
    source, metric, base_velocity, drop_elem, drop_coord, drop_vel, drop_prop, drop_counts
):
    slabs = lax.axis_size("stream")
    cols = lax.axis_size("cross")
    lanes = source.shape[-1]
    reach, capacity = drop_elem.shape[2:]
    elem_z = metric.shape[-1]
    vmem = pl.BlockSpec(memory_space=pltpu.VMEM)
    smem = pl.BlockSpec(memory_space=pltpu.SMEM)
    tiles = jnp.asarray(table_tiles(lanes))
    stiff_w = jnp.asarray(lane_weights(STIFF, lanes, True))
    deriv_w = jnp.asarray(lane_weights(DERIV, lanes, False))
    to_lanes = np.zeros((lanes, lanes))
    to_lanes[:elem_z] = np.kron(np.eye(elem_z), np.ones((1, NODES)))
    spread_w = jnp.asarray(np.concatenate([to_lanes, to_lanes], 0), BF16)

    first, own, *routed = pl.pallas_call(
        lambda *refs: pack_kernel(cols, elem_z, *refs),
        out_shape=[near(NODES + 1, NODES, lanes)] + [near(2, NODES, capacity)] * 5,
        in_specs=[vmem] * 6 + [smem],
        out_specs=[vmem] * 6,
        scratch_shapes=[pltpu.VMEM((reach, 2, NODES, capacity), F32)],
        name="pack",
    )(
        source,
        metric,
        drop_elem.reshape(reach, 1, capacity),
        drop_coord.reshape(3 * reach, 1, capacity),
        drop_vel.reshape(3 * reach, 1, capacity),
        drop_prop,
        drop_counts,
    )
    whole = ("stream", "cross")

    routed = [
        lax.ppermute(value, whole, neighbours(slabs, cols, *route))
        for value, route in zip(routed, ROUTES)
    ]
    from_source = lax.ppermute(source, whole, swapped_bit(slabs, cols, 1))
    from_metric = lax.ppermute(metric, whole, swapped_bit(slabs, cols, 1))
    gathered = pl.pallas_call(
        near_kernel,
        out_shape=near(2, NODES + 1, NODES, lanes),
        in_specs=[vmem] * 3,
        out_specs=vmem,
        name="near_pair",
    )(held(first), held(from_source), held(from_metric))
    gathered = jnp.concatenate(
        [gathered, lax.ppermute(gathered, whole, swapped_bit(slabs, cols, 2))], 0
    )
    to_far = pl.pallas_call(
        far_kernel,
        out_shape=[near(F_COUNT, NODES, lanes)] * 2,
        in_specs=[vmem],
        out_specs=[vmem] * 2,
        name="far_records",
    )(held(gathered))
    pieces = [gathered] + [
        lax.ppermute(value, whole, neighbours(slabs, cols, DEPTH, odd, 1))
        for odd, value in enumerate(to_far)
    ]
    columns = [pieces]
    bit = 1
    while bit < cols:
        columns = columns + [
            [lax.ppermute(piece, "cross", column_pairs(cols, bit)) for piece in group]
            for group in columns
        ]
        bit *= 2
    flat = [piece for group in columns for piece in group]

    span = 2 * DEPTH - 1
    field = (cols, NODES, NODES, lanes)
    scratch_bytes = 4 * (9 * DEPTH + 1 + 5 * span) * int(np.prod(field))
    pressure, momentum, face_even, face_odd, *accels = pl.pallas_call(
        lambda *refs: main_kernel(slabs, cols, *refs),
        out_shape=[f32(NODES, NODES, lanes), near(3, NODES, NODES, lanes)]
        + [near(3, NODES, lanes)] * 2
        + [near(NODES, capacity)] * 5,
        in_specs=[vmem] * (10 + 3 * cols),
        out_specs=[vmem] * 9,
        scratch_shapes=[
            pltpu.VMEM((4 * DEPTH - 1,) + field, F32),
            pltpu.VMEM((4 * DEPTH - 1, cols, NODES, lanes), F32),
            pltpu.VMEM((span,) + field, F32),
            pltpu.VMEM((span,) + field, F32),
            pltpu.VMEM((span,) + field, F32),
            pltpu.VMEM((span + 2,) + field, F32),
            pltpu.VMEM((5, span + 2, cols, NODES, lanes), F32),
            pltpu.VMEM((span + 2, cols, 2, NODES, lanes), F32),
        ],
        compiler_params=pltpu.CompilerParams(vmem_limit_bytes=2 * scratch_bytes + 2**23),
        name="sweeps_and_droplets",
    )(
        tiles,
        stiff_w,
        deriv_w,
        spread_w,
        *[held(piece) for piece in flat],
        base_velocity,
        held(own),
        *[held(value) for value in routed],
    )
    acc_own, acc_e1, acc_o1, acc_e2, acc_o2 = accels

    got_e2, got_o2 = [
        lax.ppermute(value, whole, neighbours(slabs, cols, *route))
        for value, route in zip((acc_e2, acc_o2), ROUTES[2:])
    ]
    face_even = lax.ppermute(face_even, "cross", side_pairs(cols, 0))
    if cols > 2:
        face_odd = lax.ppermute(face_odd, "cross", side_pairs(cols, 1))
    momentum, send_e1, send_o1 = pl.pallas_call(
        lambda *refs: middle_kernel(cols, *refs),
        out_shape=[near(3, NODES, NODES, lanes)] + [near(4, NODES, lanes)] * 2,
        in_specs=[vmem] * 5,
        out_specs=[vmem] * 3,
        name="cross_faces",
    )(*[held(value) for value in (momentum, face_even, face_odd, acc_e1, acc_o1)])
    got_e1, got_o1 = [
        lax.ppermute(value, whole, neighbours(slabs, cols, *route))
        for value, route in zip((send_e1, send_o1), ROUTES[:2])
    ]
    momentum, accel = pl.pallas_call(
        lambda *refs: last_kernel(slabs, reach, *refs),
        out_shape=[f32(3, NODES, NODES, lanes), f32(3 * reach, 1, capacity)],
        in_specs=[vmem] * 6,
        out_specs=[vmem] * 2,
        name="stream_faces",
    )(*[held(value) for value in (momentum, got_e1, got_o1, acc_own, got_e2, got_o2)])
    return (pressure, momentum, accel.reshape(1, 1, reach, 3, capacity))


def solution(mesh):
    in_specs = (
        P("stream", "cross", None),
        P("stream", "cross", None),
        P(None, "stream", "cross", None),
        P("stream", "cross", None, None),
        P("stream", "cross", None, None, None),
        P("stream", "cross", None, None, None),
        P("stream", "cross", None, None, None),
        P("stream", "cross", None),
    )
    out_specs = (
        P("stream", "cross", None),
        P(None, "stream", "cross", None),
        P("stream", "cross", None, None, None),
    )
    return jax.shard_map(step, mesh=mesh, in_specs=in_specs, out_specs=out_specs, check_vma=False)
```

profile of v0, /device:TPU:8, one launch (start us, length us, event | category | flops | bytes accessed | tf_op | source)
XLA Modules:
  0.0 39.6 jit_solution(13505055617637581391)
XLA Ops:
  0.6 1.0 %collective-permute-start = (f32[8,8,128]{2,1,0:T(8,128)}, f32[8,8,128]{2,1,0:T(8,128)S(1)}, u32[]{:S(2)}, u32[]{:S(2)}) collective-permute-start(f32[8,8,128]{2,1,0:T(8,128)} %refs_0_.2), channel_id=1, source_target_pairs={{0,3},{1,2},{2,1},{3,0},{4,7},{5,6},{6,5},{7,4},{8,11},{9,10},{10,... | collective-permute-start | bytes 98312 | tf_op jit(solution)/shard_map/ppermute | solution.py:627
  1.6 0.8 %collective-permute-start.1 = (f32[1,1,16]{2,1,0:T(1,128)}, f32[1,1,16]{2,1,0:T(1,128)S(1)}, u32[]{:S(2)}, u32[]{:S(2)}) collective-permute-start(f32[1,1,16]{2,1,0:T(1,128)} %refs_1_.2), channel_id=1, source_target_pairs={{0,3},{1,2},{2,1},{3,0},{4,7},{5,6},{6,5},{7,4},{8,11},{9,10},{10,... | collective-permute-start | bytes 200 | tf_op jit(solution)/shard_map/ppermute | solution.py:628
  2.4 0.8 %pack.1 = (f32[9,8,128]{2,1,0:T(8,128)S(1)}, f32[2,8,128]{2,1,0:T(8,128)S(1)}, f32[2,8,128]{2,1,0:T(8,128)S(1)}, f32[2,8,128]{2,1,0:T(8,128)S(1)}, f32[2,8,128]{2,1,0:T(8,128)S(1)}, /*index=5*/f32[2,8,128]{2,1,0:T(8,128)S(1)}) custom-call(f32[8,8,128]{2,1,0:T(8,128)} %refs_0_.2, f32[1,1,16]{2,1,0:T(1,128)} %refs_1_.2, s32[5,1,128]{2,1,0:T(1,128)} %bitcast.8, ...), custom_call_target="tpu_custom_call" | custom-call | tf_op jit(solution)/shard_map/pack/pallas_call | solution.py:605
  3.3 1.5 %collective-permute-done.1.from_metric = f32[1,1,16]{2,1,0:T(1,128)S(1)} collective-permute-done((f32[1,1,16]{2,1,0:T(1,128)}, f32[1,1,16]{2,1,0:T(1,128)S(1)}, u32[]{:S(2)}, u32[]{:S(2)}) %collective-permute-start.1) | collective-permute-done | bytes 96 | tf_op jit(solution)/shard_map/ppermute | solution.py:628
  4.8 0.0 collective-permute-done.from_source
  4.8 0.0 copy-start.3
  4.8 0.0 copy-start.4
  4.8 1.9 %collective-permute-start.2 = (f32[2,9,8,128]{3,2,1,0:T(8,128)S(1)}, f32[2,9,8,128]{3,2,1,0:T(8,128)S(1)}, u32[]{:S(2)}, u32[]{:S(2)}) collective-permute-start(f32[2,9,8,128]{3,2,1,0:T(8,128)S(1)} %near_pair.1), channel_id=1, source_target_pairs={{0,5},{1,4},{2,7},{3,6},{4,1},{5,0},{6,3},{7,2},{8,13},{9,12},{10,... | collective-permute-start | bytes 221192 | tf_op jit(solution)/shard_map/ppermute | solution.py:637
  6.6 2.0 %collective-permute-done.2 = f32[2,9,8,128]{3,2,1,0:T(8,128)S(1)} collective-permute-done((f32[2,9,8,128]{3,2,1,0:T(8,128)S(1)}, f32[2,9,8,128]{3,2,1,0:T(8,128)S(1)}, u32[]{:S(2)}, u32[]{:S(2)}) %collective-permute-start.2) | collective-permute-done | bytes 73760 | tf_op jit(solution)/shard_map/ppermute | solution.py:637
  8.7 0.0 copy-start.1
  8.7 0.0 copy-start.2
  8.7 0.0 copy-start
  8.7 0.7 %collective-permute-start.3 = (f32[26,8,128]{2,1,0:T(8,128)S(1)}, f32[26,8,128]{2,1,0:T(8,128)S(1)}, u32[]{:S(2)}, u32[]{:S(2)}) collective-permute-start(f32[26,8,128]{2,1,0:T(8,128)S(1)} %get-tuple-element.26), channel_id=1, source_target_pairs={{0,9},{1,8},{2,11},{3,10},{4,13},{5,12},{6,15},{7,14},{8,1},{9,0},... | collective-permute-start | bytes 319496 | tf_op jit(solution)/shard_map/ppermute | solution.py:647
  9.5 2.2 %collective-permute-start.4 = (f32[26,8,128]{2,1,0:T(8,128)S(1)}, f32[26,8,128]{2,1,0:T(8,128)S(1)}, u32[]{:S(2)}, u32[]{:S(2)}) collective-permute-start(f32[26,8,128]{2,1,0:T(8,128)S(1)} %get-tuple-element.27), channel_id=1, source_target_pairs={{0,1},{1,0},{2,3},{3,2},{4,5},{5,4},{6,7},{7,6},{8,17},{9,16},{10,... | collective-permute-start | bytes 319496 | tf_op jit(solution)/shard_map/ppermute | solution.py:647
  11.7 0.6 %collective-permute-start.5 = (f32[4,9,8,128]{3,2,1,0:T(8,128)S(1)}, f32[4,9,8,128]{3,2,1,0:T(8,128)S(1)}, u32[]{:S(2)}, u32[]{:S(2)}) collective-permute-start(f32[4,9,8,128]{3,2,1,0:T(8,128)S(1)} %pad_maximum_fusion.gathered.refs_4_), channel_id=1, source_target_pairs={{0,1},{1,0},{2,3},{3,2},{4,5},{5,4},{6,7},{7,6},{8,9},{9,8},{10,11... | collective-permute-start | bytes 442376 | tf_op jit(solution)/shard_map/ppermute | solution.py:654
  12.3 1.0 %collective-permute-done.3.refs_5_ = f32[26,8,128]{2,1,0:T(8,128)S(1)} collective-permute-done((f32[26,8,128]{2,1,0:T(8,128)S(1)}, f32[26,8,128]{2,1,0:T(8,128)S(1)}, u32[]{:S(2)}, u32[]{:S(2)}) %collective-permute-start.3) | collective-permute-done | bytes 106528 | tf_op jit(solution)/shard_map/ppermute | solution.py:647
  13.3 0.9 %collective-permute-start.6 = (f32[26,8,128]{2,1,0:T(8,128)S(1)}, f32[26,8,128]{2,1,0:T(8,128)S(1)}, u32[]{:S(2)}, u32[]{:S(2)}) collective-permute-start(f32[26,8,128]{2,1,0:T(8,128)S(1)} %collective-permute-done.3.refs_5_), channel_id=1, source_target_pairs={{0,1},{1,0},{2,3},{3,2},{4,5},{5,4},{6,7},{7,6},{8,9},{9,8},{10,11... | collective-permute-start | bytes 319496 | tf_op jit(solution)/shard_map/ppermute | solution.py:654
  14.2 0.8 %collective-permute-done.4.refs_6_ = f32[26,8,128]{2,1,0:T(8,128)S(1)} collective-permute-done((f32[26,8,128]{2,1,0:T(8,128)S(1)}, f32[26,8,128]{2,1,0:T(8,128)S(1)}, u32[]{:S(2)}, u32[]{:S(2)}) %collective-permute-start.4) | collective-permute-done | bytes 106528 | tf_op jit(solution)/shard_map/ppermute | solution.py:647
  15.0 0.0 collective-permute-start.7
  15.0 1.9 %collective-permute-start.8 = (f32[2,8,128]{2,1,0:T(8,128)S(1)}, f32[2,8,128]{2,1,0:T(8,128)S(1)}, u32[]{:S(2)}, u32[]{:S(2)}) collective-permute-start(f32[2,8,128]{2,1,0:T(8,128)S(1)} %get-tuple-element.29), channel_id=1, source_target_pairs={{0,2},{1,3},{2,0},{3,1},{4,6},{5,7},{6,4},{7,5},{8,10},{9,11},{10,... | collective-permute-start | bytes 24584 | tf_op jit(solution)/shard_map/ppermute | solution.py:624
  17.0 0.1 collective-permute-start.9
  17.1 1.6 %collective-permute-done.8.refs_12_ = f32[2,8,128]{2,1,0:T(8,128)S(1)} collective-permute-done((f32[2,8,128]{2,1,0:T(8,128)S(1)}, f32[2,8,128]{2,1,0:T(8,128)S(1)}, u32[]{:S(2)}, u32[]{:S(2)}) %collective-permute-start.8) | collective-permute-done | bytes 8224 | tf_op jit(solution)/shard_map/ppermute | solution.py:624
  18.7 1.6 %collective-permute-start.10 = (f32[2,8,128]{2,1,0:T(8,128)S(1)}, f32[2,8,128]{2,1,0:T(8,128)S(1)}, u32[]{:S(2)}, u32[]{:S(2)}) collective-permute-start(f32[2,8,128]{2,1,0:T(8,128)S(1)} %get-tuple-element.31), channel_id=1, source_target_pairs={{0,4},{1,5},{2,6},{3,7},{4,0},{5,1},{6,2},{7,3},{8,12},{9,13},{10,... | collective-permute-start | bytes 24584 | tf_op jit(solution)/shard_map/ppermute | solution.py:624
  20.2 2.2 %collective-permute-done.9.refs_13_ = f32[2,8,128]{2,1,0:T(8,128)S(1)} collective-permute-done((f32[2,8,128]{2,1,0:T(8,128)S(1)}, f32[2,8,128]{2,1,0:T(8,128)S(1)}, u32[]{:S(2)}, u32[]{:S(2)}) %collective-permute-start.9) | collective-permute-done | bytes 8224 | tf_op jit(solution)/shard_map/ppermute | solution.py:624
  22.4 0.0 collective-permute-start.11
  22.4 0.0 collective-permute-done.10.refs_14_
  22.4 4.5 %collective-permute-done.11.refs_15_ = f32[2,8,128]{2,1,0:T(8,128)S(1)} collective-permute-done((f32[2,8,128]{2,1,0:T(8,128)S(1)}, f32[2,8,128]{2,1,0:T(8,128)S(1)}, u32[]{:S(2)}, u32[]{:S(2)}) %collective-permute-start.11) | collective-permute-done | bytes 8224 | tf_op jit(solution)/shard_map/ppermute | solution.py:624
  27.0 0.0 collective-permute-done.5.refs_7_
  27.0 0.0 collective-permute-done.6.refs_8_
  27.0 0.0 collective-permute-done.7.refs_9_
  27.0 0.0 copy-done.3
  27.0 0.0 copy-done.4
  27.0 0.0 copy-done.1
  27.0 0.0 copy-done.2
  27.0 0.0 copy-done
  27.0 2.6 %sweeps_and_droplets.1 = (f32[8,8,128]{2,1,0:T(8,128)}, f32[3,8,8,128]{3,2,1,0:T(8,128)S(1)}, f32[3,8,128]{2,1,0:T(8,128)S(1)}, f32[3,8,128]{2,1,0:T(8,128)S(1)}...) custom-call(f32[33,8,128]{2,1,0:T(8,128)S(1)} %copy-done, ...), custom_call_target="tpu_custom_call" | custom-call | tf_op jit(solution)/shard_map/sweeps_and_droplets/pallas_call | solution.py:663
  29.6 0.0 collective-permute-start.12
  29.6 1.2 %collective-permute-done.12.refs_1_ = f32[3,8,128]{2,1,0:T(8,128)S(1)} collective-permute-done((f32[3,8,128]{2,1,0:T(8,128)S(1)}, f32[3,8,128]{2,1,0:T(8,128)S(1)}, u32[]{:S(2)}, u32[]{:S(2)}) %collective-permute-start.12) | collective-permute-done | bytes 12320 | tf_op jit(solution)/shard_map/ppermute | solution.py:698
  30.9 0.1 collective-permute-start.13
  30.9 1.5 %collective-permute-start.14 = (f32[4,8,128]{2,1,0:T(8,128)S(1)}, f32[4,8,128]{2,1,0:T(8,128)S(1)}, u32[]{:S(2)}, u32[]{:S(2)}) collective-permute-start(f32[4,8,128]{2,1,0:T(8,128)S(1)} %get-tuple-element.41), channel_id=1, source_target_pairs={{0,1},{1,0},{2,4},{3,5},{4,2},{5,3},{6,8},{7,9},{8,6},{9,7},{10,12... | collective-permute-start | bytes 49160 | tf_op jit(solution)/shard_map/ppermute | solution.py:709
  32.4 2.0 %collective-permute-start.15 = (f32[8,128]{1,0:T(8,128)S(1)}, f32[8,128]{1,0:T(8,128)S(1)}, u32[]{:S(2)}, u32[]{:S(2)}) collective-permute-start(f32[8,128]{1,0:T(8,128)S(1)} %get-tuple-element.43), channel_id=1, source_target_pairs={{0,4},{1,5},{2,6},{3,7},{4,0},{5,1},{6,2},{7,3},{8,12},{9,13},{10,... | collective-permute-start | bytes 12296 | tf_op jit(solution)/shard_map/ppermute | solution.py:695
  34.4 0.0 collective-permute-start.16
  34.4 1.6 %collective-permute-done.15.refs_4_ = f32[8,128]{1,0:T(8,128)S(1)} collective-permute-done((f32[8,128]{1,0:T(8,128)S(1)}, f32[8,128]{1,0:T(8,128)S(1)}, u32[]{:S(2)}, u32[]{:S(2)}) %collective-permute-start.15) | collective-permute-done | bytes 4128 | tf_op jit(solution)/shard_map/ppermute | solution.py:695
  36.0 2.9 %collective-permute-done.16.refs_5_ = f32[8,128]{1,0:T(8,128)S(1)} collective-permute-done((f32[8,128]{1,0:T(8,128)S(1)}, f32[8,128]{1,0:T(8,128)S(1)}, u32[]{:S(2)}, u32[]{:S(2)}) %collective-permute-start.16) | collective-permute-done | bytes 4128 | tf_op jit(solution)/shard_map/ppermute | solution.py:695
  38.9 0.0 collective-permute-done.13.refs_1_
  38.9 0.0 collective-permute-done.14.refs_2_
  38.9 0.7 %stream_faces.1 = (f32[3,8,8,128]{3,2,1,0:T(8,128)}, f32[15,1,128]{2,1,0:T(1,128)}) custom-call(f32[3,8,8,128]{3,2,1,0:T(8,128)S(1)} %get-tuple-element.39.refs_0_, f32[4,8,128]{2,1,0:T(8,128)S(1)} %collective-permute-done.13.refs_1_, f32[4,8,128]{2,1,0:T(8,128)S(1)} %collective-permute-done.14.refs_2_, f32[8,128]{1,0:T(8,128)S(1)} %get-tuple-element.42.refs_3_, ...), custom_call_target="tpu_custom_call" | custom-call | tf_op jit(solution)/shard_map/stream_faces/pallas_call | solution.py:712
  (4 shorter events, 0.1 us)
Async XLA Ops:
  0.6 4.1 %collective-permute-start = (f32[8,8,128]{2,1,0:T(8,128)}, f32[8,8,128]{2,1,0:T(8,128)S(1)}, u32[]{:S(2)}, u32[]{:S(2)}) collective-permute-start(f32[8,8,128]{2,1,0:T(8,128)} %refs_0_.2), channel_id=1, source_target_pairs={{0,3},{1,2},{2,1},{3,0},{4,7},{5,6},{6,5},{7,4},{8,11},{9,10},{10,... | collective-permute-start | bytes 98312 | tf_op jit(solution)/shard_map/ppermute | solution.py:627
  1.6 3.1 %collective-permute-start.1 = (f32[1,1,16]{2,1,0:T(1,128)}, f32[1,1,16]{2,1,0:T(1,128)S(1)}, u32[]{:S(2)}, u32[]{:S(2)}) collective-permute-start(f32[1,1,16]{2,1,0:T(1,128)} %refs_1_.2), channel_id=1, source_target_pairs={{0,3},{1,2},{2,1},{3,0},{4,7},{5,6},{6,5},{7,4},{8,11},{9,10},{10,... | collective-permute-start | bytes 200 | tf_op jit(solution)/shard_map/ppermute | solution.py:628
  4.8 22.2 %copy-start.3 = (f32[3,8,8,128]{3,2,1,0:T(8,128)S(1)}, f32[3,8,8,128]{3,2,1,0:T(8,128)}, u32[]{:S(2)}) copy-start(f32[3,8,8,128]{3,2,1,0:T(8,128)} %refs_10_.1) | copy-start | bytes 294916
  4.8 22.2 %copy-start.4 = (bf16[256,128]{1,0:T(8,128)(2,1)S(1)}, bf16[256,128]{1,0:T(8,128)(2,1)}, u32[]{:S(2)}) copy-start(bf16[256,128]{1,0:T(8,128)(2,1)} %constant.11.clone.refs_3_) | copy-start | bytes 196612
  4.8 3.9 %collective-permute-start.2 = (f32[2,9,8,128]{3,2,1,0:T(8,128)S(1)}, f32[2,9,8,128]{3,2,1,0:T(8,128)S(1)}, u32[]{:S(2)}, u32[]{:S(2)}) collective-permute-start(f32[2,9,8,128]{3,2,1,0:T(8,128)S(1)} %near_pair.1), channel_id=1, source_target_pairs={{0,5},{1,4},{2,7},{3,6},{4,1},{5,0},{6,3},{7,2},{8,13},{9,12},{10,... | collective-permute-start | bytes 221192 | tf_op jit(solution)/shard_map/ppermute | solution.py:637
  8.7 18.3 %copy-start.1 = (bf16[256,256]{1,0:T(8,128)(2,1)S(1)}, bf16[256,256]{1,0:T(8,128)(2,1)}, u32[]{:S(2)}) copy-start(bf16[256,256]{1,0:T(8,128)(2,1)} %constant.10.clone.refs_2_) | copy-start | bytes 393220
  8.7 18.3 %copy-start.2 = (bf16[256,256]{1,0:T(8,128)(2,1)S(1)}, bf16[256,256]{1,0:T(8,128)(2,1)}, u32[]{:S(2)}) copy-start(bf16[256,256]{1,0:T(8,128)(2,1)} %constant.9.clone.refs_1_) | copy-start | bytes 393220
  8.7 18.3 %copy-start = (f32[33,8,128]{2,1,0:T(8,128)S(1)}, f32[33,8,128]{2,1,0:T(8,128)}, u32[]{:S(2)}) copy-start(f32[33,8,128]{2,1,0:T(8,128)} %constant.8.clone.refs_0_) | copy-start | bytes 405508
  8.7 4.5 %collective-permute-start.3 = (f32[26,8,128]{2,1,0:T(8,128)S(1)}, f32[26,8,128]{2,1,0:T(8,128)S(1)}, u32[]{:S(2)}, u32[]{:S(2)}) collective-permute-start(f32[26,8,128]{2,1,0:T(8,128)S(1)} %get-tuple-element.26), channel_id=1, source_target_pairs={{0,9},{1,8},{2,11},{3,10},{4,13},{5,12},{6,15},{7,14},{8,1},{9,0},... | collective-permute-start | bytes 319496 | tf_op jit(solution)/shard_map/ppermute | solution.py:647
  9.5 5.5 %collective-permute-start.4 = (f32[26,8,128]{2,1,0:T(8,128)S(1)}, f32[26,8,128]{2,1,0:T(8,128)S(1)}, u32[]{:S(2)}, u32[]{:S(2)}) collective-permute-start(f32[26,8,128]{2,1,0:T(8,128)S(1)} %get-tuple-element.27), channel_id=1, source_target_pairs={{0,1},{1,0},{2,3},{3,2},{4,5},{5,4},{6,7},{7,6},{8,17},{9,16},{10,... | collective-permute-start | bytes 319496 | tf_op jit(solution)/shard_map/ppermute | solution.py:647
  11.7 15.3 %collective-permute-start.5 = (f32[4,9,8,128]{3,2,1,0:T(8,128)S(1)}, f32[4,9,8,128]{3,2,1,0:T(8,128)S(1)}, u32[]{:S(2)}, u32[]{:S(2)}) collective-permute-start(f32[4,9,8,128]{3,2,1,0:T(8,128)S(1)} %pad_maximum_fusion.gathered.refs_4_), channel_id=1, source_target_pairs={{0,1},{1,0},{2,3},{3,2},{4,5},{5,4},{6,7},{7,6},{8,9},{9,8},{10,11... | collective-permute-start | bytes 442376 | tf_op jit(solution)/shard_map/ppermute | solution.py:654
  13.3 13.7 %collective-permute-start.6 = (f32[26,8,128]{2,1,0:T(8,128)S(1)}, f32[26,8,128]{2,1,0:T(8,128)S(1)}, u32[]{:S(2)}, u32[]{:S(2)}) collective-permute-start(f32[26,8,128]{2,1,0:T(8,128)S(1)} %collective-permute-done.3.refs_5_), channel_id=1, source_target_pairs={{0,1},{1,0},{2,3},{3,2},{4,5},{5,4},{6,7},{7,6},{8,9},{9,8},{10,11... | collective-permute-start | bytes 319496 | tf_op jit(solution)/shard_map/ppermute | solution.py:654
  15.0 12.0 %collective-permute-start.7 = (f32[26,8,128]{2,1,0:T(8,128)S(1)}, f32[26,8,128]{2,1,0:T(8,128)S(1)}, u32[]{:S(2)}, u32[]{:S(2)}) collective-permute-start(f32[26,8,128]{2,1,0:T(8,128)S(1)} %collective-permute-done.4.refs_6_), channel_id=1, source_target_pairs={{0,1},{1,0},{2,3},{3,2},{4,5},{5,4},{6,7},{7,6},{8,9},{9,8},{10,11... | collective-permute-start | bytes 319496 | tf_op jit(solution)/shard_map/ppermute | solution.py:654
  15.0 3.7 %collective-permute-start.8 = (f32[2,8,128]{2,1,0:T(8,128)S(1)}, f32[2,8,128]{2,1,0:T(8,128)S(1)}, u32[]{:S(2)}, u32[]{:S(2)}) collective-permute-start(f32[2,8,128]{2,1,0:T(8,128)S(1)} %get-tuple-element.29), channel_id=1, source_target_pairs={{0,2},{1,3},{2,0},{3,1},{4,6},{5,7},{6,4},{7,5},{8,10},{9,11},{10,... | collective-permute-start | bytes 24584 | tf_op jit(solution)/shard_map/ppermute | solution.py:624
  17.0 5.5 %collective-permute-start.9 = (f32[2,8,128]{2,1,0:T(8,128)S(1)}, f32[2,8,128]{2,1,0:T(8,128)S(1)}, u32[]{:S(2)}, u32[]{:S(2)}) collective-permute-start(f32[2,8,128]{2,1,0:T(8,128)S(1)} %get-tuple-element.30), channel_id=1, source_target_pairs={{0,1},{1,0},{2,4},{3,5},{4,2},{5,3},{6,8},{7,9},{8,6},{9,7},{10,12... | collective-permute-start | bytes 24584 | tf_op jit(solution)/shard_map/ppermute | solution.py:624
  18.7 3.7 %collective-permute-start.10 = (f32[2,8,128]{2,1,0:T(8,128)S(1)}, f32[2,8,128]{2,1,0:T(8,128)S(1)}, u32[]{:S(2)}, u32[]{:S(2)}) collective-permute-start(f32[2,8,128]{2,1,0:T(8,128)S(1)} %get-tuple-element.31), channel_id=1, source_target_pairs={{0,4},{1,5},{2,6},{3,7},{4,0},{5,1},{6,2},{7,3},{8,12},{9,13},{10,... | collective-permute-start | bytes 24584 | tf_op jit(solution)/shard_map/ppermute | solution.py:624
  22.4 4.5 %collective-permute-start.11 = (f32[2,8,128]{2,1,0:T(8,128)S(1)}, f32[2,8,128]{2,1,0:T(8,128)S(1)}, u32[]{:S(2)}, u32[]{:S(2)}) collective-permute-start(f32[2,8,128]{2,1,0:T(8,128)S(1)} %get-tuple-element.32), channel_id=1, source_target_pairs={{0,1},{1,0},{2,3},{3,2},{4,8},{5,9},{6,10},{7,11},{8,4},{9,5},{10,... | collective-permute-start | bytes 24584 | tf_op jit(solution)/shard_map/ppermute | solution.py:624
  29.6 1.2 %collective-permute-start.12 = (f32[3,8,128]{2,1,0:T(8,128)S(1)}, f32[3,8,128]{2,1,0:T(8,128)S(1)}, u32[]{:S(2)}, u32[]{:S(2)}) collective-permute-start(f32[3,8,128]{2,1,0:T(8,128)S(1)} %get-tuple-element.35), channel_id=1, source_target_pairs={{0,1},{1,0},{2,3},{3,2},{4,5},{5,4},{6,7},{7,6},{8,9},{9,8},{10,11... | collective-permute-start | bytes 36872 | tf_op jit(solution)/shard_map/ppermute | solution.py:698
  30.9 8.1 %collective-permute-start.13 = (f32[4,8,128]{2,1,0:T(8,128)S(1)}, f32[4,8,128]{2,1,0:T(8,128)S(1)}, u32[]{:S(2)}, u32[]{:S(2)}) collective-permute-start(f32[4,8,128]{2,1,0:T(8,128)S(1)} %get-tuple-element.40), channel_id=1, source_target_pairs={{0,2},{1,3},{2,0},{3,1},{4,6},{5,7},{6,4},{7,5},{8,10},{9,11},{10,... | collective-permute-start | bytes 49160 | tf_op jit(solution)/shard_map/ppermute | solution.py:709
  30.9 8.0 %collective-permute-start.14 = (f32[4,8,128]{2,1,0:T(8,128)S(1)}, f32[4,8,128]{2,1,0:T(8,128)S(1)}, u32[]{:S(2)}, u32[]{:S(2)}) collective-permute-start(f32[4,8,128]{2,1,0:T(8,128)S(1)} %get-tuple-element.41), channel_id=1, source_target_pairs={{0,1},{1,0},{2,4},{3,5},{4,2},{5,3},{6,8},{7,9},{8,6},{9,7},{10,12... | collective-permute-start | bytes 49160 | tf_op jit(solution)/shard_map/ppermute | solution.py:709
  32.4 3.6 %collective-permute-start.15 = (f32[8,128]{1,0:T(8,128)S(1)}, f32[8,128]{1,0:T(8,128)S(1)}, u32[]{:S(2)}, u32[]{:S(2)}) collective-permute-start(f32[8,128]{1,0:T(8,128)S(1)} %get-tuple-element.43), channel_id=1, source_target_pairs={{0,4},{1,5},{2,6},{3,7},{4,0},{5,1},{6,2},{7,3},{8,12},{9,13},{10,... | collective-permute-start | bytes 12296 | tf_op jit(solution)/shard_map/ppermute | solution.py:695
  34.4 4.5 %collective-permute-start.16 = (f32[8,128]{1,0:T(8,128)S(1)}, f32[8,128]{1,0:T(8,128)S(1)}, u32[]{:S(2)}, u32[]{:S(2)}) collective-permute-start(f32[8,128]{1,0:T(8,128)S(1)} %get-tuple-element.44), channel_id=1, source_target_pairs={{0,1},{1,0},{2,3},{3,2},{4,8},{5,9},{6,10},{7,11},{8,4},{9,5},{10,... | collective-permute-start | bytes 12296 | tf_op jit(solution)/shard_map/ppermute | solution.py:695
where the time goes:
time: 39.9 us; the launch traced here: 39.6 us
  waiting for transfers between devices  19.3 us (48%)
  starting transfers between devices  15.3 us (38%)
  Pallas kernels  4.19 us (11%)
  between operations  0.74 us (2%)
    ppermute x8, waiting for transfers between devices, step(): lax.ppermute(value, whole, neighbours(slabs, cols, *route))  12.8 us
    ppermute x8, starting transfers between devices, step(): lax.ppermute(value, whole, neighbours(slabs, cols, *route))  7.15 us
    ppermute x2, starting transfers between devices, step(): lax.ppermute(value, whole, neighbours(slabs, cols, DEPTH, odd, 1))  2.94 us
    pallas_call x1, Pallas kernels, step(): pl.pallas_call(lambda *refs: main_kernel(slabs, cols, *refs), out_shape=[...  2.59 us
    ppermute x1, waiting for transfers between devices, step(): lax.ppermute(gathered, whole, swapped_bit(slabs, cols, 2))  2.04 us
    ppermute x1, starting transfers between devices, step(): lax.ppermute(gathered, whole, swapped_bit(slabs, cols, 2))  1.87 us
    ppermute x2, waiting for transfers between devices, step(): lax.ppermute(value, whole, neighbours(slabs, cols, DEPTH, odd, 1))  1.78 us
    ppermute x3, starting transfers between devices, step(): lax.ppermute(piece, 'cross', column_pairs(cols, bit))  1.57 us
  transfers between devices with their start and end apart: 17, of which 10 were waited for; matrix products, arithmetic and copies ran while one was open for 0% of the time, Pallas kernels for 2%

commit v1 on v0

--- a/solution.py
+++ b/solution.py
@@ -305,13 +305,34 @@
     return factor
 
 
+def basis_kernel(slabs, tiles, own, *rest):
+    routed, (high, low, cells, live) = rest[:4], rest[4:]
+    position = lax.axis_index("stream")
+    lanes, capacity = tiles.shape[-1], own.shape[-1]
+    opened = [None] + [route_open(position, route, slabs) for route in ROUTES]
+    for g, (group, there) in enumerate(zip((own,) + tuple(routed), opened)):
+        ids = group[1]
+        if there is not None:
+            ids = jnp.where(there, ids, 0.0)
+        live[g] = ids
+        basis = [lagrange(group[0, axis : axis + 1, :], tiles) for axis in range(3)]
+        pick = jnp.concatenate(
+            [jnp.where(ids == float(e + 1), basis[2], 0.0) for e in range(lanes // NODES)], 0
+        )
+        place = slice(g * capacity, (g + 1) * capacity)
+        high[:, place], low[:, place] = split_value(pick)
+        for i in range(NODES):
+            cells[g, i] = basis[1] * basis[0][i : i + 1, :]
+
+
 def main_kernel(slabs, cols, *refs):
     tiles, stiff_w, deriv_w, spread_w = refs[0:4]
     pieces = refs[4 : 4 + 3 * cols]
     base_velocity, own = refs[4 + 3 * cols : 6 + 3 * cols]
     routed = refs[6 + 3 * cols : 10 + 3 * cols]
-    (pressure, momentum, face_even, face_odd, acc_own, acc_e1, acc_o1, acc_e2, acc_o2,
-     loads, scales, resid, update, inv, work, spans, layers) = refs[10 + 3 * cols :]
+    picks_high, picks_low, cells_ref, live = refs[10 + 3 * cols : 14 + 3 * cols]
+    (pressure, momentum, face_even, acc_own, acc_e1, acc_o1, acc_e2, acc_o2,
+     *face_odd, loads, scales, resid, update, inv, work, spans, layers) = refs[14 + 3 * cols :]
     lanes = tiles.shape[-1]
     position = lax.axis_index("stream")
     column = lax.axis_index("cross")
@@ -482,17 +503,7 @@
         velocity.append(base_velocity[2, i] - scale * grad_z[i])
     velocity = jnp.concatenate(velocity, 0)
 
-    groups = [(own[0], own[1])]
-    for route, group in zip(ROUTES, routed):
-        groups.append((group[0], jnp.where(route_open(position, route, slabs), group[1], 0.0)))
-    pick, bases = [], []
-    for group, ids in groups:
-        basis = [lagrange(group[axis : axis + 1, :], tiles) for axis in range(3)]
-        pick.append(jnp.concatenate(
-            [jnp.where(ids == float(e + 1), basis[2], 0.0) for e in range(lanes // NODES)], 0))
-        bases.append(basis)
-    pick = jnp.concatenate(pick, 1)
-    pick_high, pick_low = split_value(pick)
+    pick_high, pick_low = picks_high[...], picks_low[...]
     vel_high, vel_low = split_value(velocity)
     partial = jnp.dot(
         jnp.concatenate([vel_high, vel_low, vel_high], 1),
@@ -501,8 +512,9 @@
     )
     capacity = own.shape[-1]
     spread = []
-    for g, ((group, ids), basis) in enumerate(zip(groups, bases)):
-        cells = [basis[1] * basis[0][i : i + 1, :] for i in range(NODES)]
+    for g, group in enumerate((own,) + tuple(routed)):
+        group, ids = group.at[0], live.at[g]
+        cells = [cells_ref[g, i] for i in range(NODES)]
         accel_rows, parts = [], []
         for comp in range(3):
             total = None
@@ -532,15 +544,16 @@
     high_row = added[:, :, NODES - 1, :]
     even = column % 2 == 0
     face_even[...] = jnp.where(even, high_row, low_row)
-    face_odd[...] = jnp.where(even, low_row, high_row)
-
-
-def middle_kernel(cols, momentum, face_even, face_odd, acc_e1, acc_o1, out, send_e1, send_o1):
+    if face_odd:
+        face_odd[0][...] = jnp.where(even, low_row, high_row)
+
+
+def middle_kernel(momentum, face_even, face_odd, acc_e1, acc_o1, out, send_e1, send_o1):
     position = lax.axis_index("stream")
     column = lax.axis_index("cross")
     even = column % 2 == 0
-    high = jnp.where(even, face_even[...], face_odd[...]) if cols > 2 else jnp.where(even, face_even[...], 0.0)
-    low = jnp.where(even, face_odd[...], face_even[...]) if cols > 2 else jnp.where(even, 0.0, face_even[...])
+    high = jnp.where(even, face_even[...], face_odd[...])
+    low = jnp.where(even, face_odd[...], face_even[...])
     out[...] = momentum[...]
     out[:, :, 0, :] = momentum[:, :, 0, :] + low
     out[:, :, NODES - 1, :] = momentum[:, :, NODES - 1, :] + high
@@ -554,7 +567,40 @@
     send_o1[3] = acc_o1[...]
 
 
-def last_kernel(slabs, reach, momentum, got_e1, got_o1, acc_own, got_e2, got_o2, out, accel):
+def bundle_kernel(momentum, face_even, acc_e1, acc_o1, acc_o2, out):
+    side = jnp.where(lax.axis_index("stream") % 2 == 0, NODES - 1, 0)
+    for comp in range(3):
+        out[comp] = face_even[comp]
+        out[3 + comp] = momentum[comp, side]
+        out[6 + comp] = momentum[comp, NODES - 1 - side]
+    out[9] = acc_e1[...]
+    out[10] = acc_o1[...]
+    out[11] = acc_o2[...]
+
+
+def exchange_kernel(momentum, got, out, send_e1, send_o1, send_o2):
+    even = lax.axis_index("cross") % 2 == 0
+    side = jnp.where(lax.axis_index("stream") % 2 == 0, NODES - 1, 0)
+    layer = got[0:3]
+    out[...] = momentum[...]
+    out[:, :, 0, :] = momentum[:, :, 0, :] + jnp.where(even, 0.0, layer)
+    out[:, :, NODES - 1, :] = momentum[:, :, NODES - 1, :] + jnp.where(even, layer, 0.0)
+    here = jnp.where(even, NODES - 1, 0)
+    there = pl.ds(NODES - 1 - here, 1)
+    for comp in range(3):
+        for send, start, at in ((send_e1, 3, side), (send_o1, 6, NODES - 1 - side)):
+            send[comp] = got[start + comp]
+            edge = momentum[comp, at, pl.ds(here, 1), :]
+            send[comp, there, :] = got[start + comp, there, :] + edge
+    send_e1[3] = got[9]
+    send_o1[3] = got[10]
+    send_o2[...] = got[11]
+
+
+def last_kernel(
+    slabs, reach, iterate, momentum, got_e1, got_o1, acc_own, got_e2, got_o2, pressure, out, accel
+):
+    pressure[...] = iterate[...]
     position = lax.axis_index("stream")
     lower = position % 2 == 0
     top = jnp.where(lower, NODES - 1, 0)
@@ -660,13 +706,23 @@
     span = 2 * DEPTH - 1
     field = (cols, NODES, NODES, lanes)
     scratch_bytes = 4 * (9 * DEPTH + 1 + 5 * span) * int(np.prod(field))
-    pressure, momentum, face_even, face_odd, *accels = pl.pallas_call(
+    slots = 5 * capacity
+    bases = pl.pallas_call(
+        lambda *refs: basis_kernel(slabs, *refs),
+        out_shape=[pltpu.VMEM((lanes, slots), BF16)] * 2
+        + [near(5, NODES, NODES, capacity), near(5, NODES, capacity)],
+        in_specs=[vmem] * 6,
+        out_specs=[vmem] * 4,
+        name="bases",
+    )(held(tiles), held(own), *[held(value) for value in routed])
+    pressure, momentum, face_even, *accels = pl.pallas_call(
         lambda *refs: main_kernel(slabs, cols, *refs),
-        out_shape=[f32(NODES, NODES, lanes), near(3, NODES, NODES, lanes)]
-        + [near(3, NODES, lanes)] * 2
-        + [near(NODES, capacity)] * 5,
-        in_specs=[vmem] * (10 + 3 * cols),
-        out_specs=[vmem] * 9,
+        out_shape=[near(NODES, NODES, lanes), near(3, NODES, NODES, lanes)]
+        + [near(3, NODES, lanes)]
+        + [near(NODES, capacity)] * 5
+        + [near(3, NODES, lanes)] * (cols > 2),
+        in_specs=[vmem] * (14 + 3 * cols),
+        out_specs=[vmem] * (8 + (cols > 2)),
         scratch_shapes=[
             pltpu.VMEM((4 * DEPTH - 1,) + field, F32),
             pltpu.VMEM((4 * DEPTH - 1, cols, NODES, lanes), F32),
@@ -687,35 +743,56 @@
         *[held(piece) for piece in flat],
         base_velocity,
         held(own),
-        *[held(value) for value in routed],
+        *[held(value) for value in (*routed, *bases)],
     )
-    acc_own, acc_e1, acc_o1, acc_e2, acc_o2 = accels
-
-    got_e2, got_o2 = [
-        lax.ppermute(value, whole, neighbours(slabs, cols, *route))
-        for value, route in zip((acc_e2, acc_o2), ROUTES[2:])
-    ]
-    face_even = lax.ppermute(face_even, "cross", side_pairs(cols, 0))
-    if cols > 2:
-        face_odd = lax.ppermute(face_odd, "cross", side_pairs(cols, 1))
-    momentum, send_e1, send_o1 = pl.pallas_call(
-        lambda *refs: middle_kernel(cols, *refs),
-        out_shape=[near(3, NODES, NODES, lanes)] + [near(4, NODES, lanes)] * 2,
-        in_specs=[vmem] * 5,
+    acc_own, acc_e1, acc_o1, acc_e2, acc_o2, *face_odd = accels
+
+    def returned(value, index, swap):
+        pairs = neighbours(slabs, cols, *ROUTES[index], swap)
+        return lax.ppermute(value, whole, pairs)
+
+    got_e2 = returned(acc_e2, 2, 0)
+    if cols == 2:
+        swap = 1
+        bundle = pl.pallas_call(
+            bundle_kernel,
+            out_shape=near(12, NODES, lanes),
+            in_specs=[vmem] * 5,
+            out_specs=vmem,
+            name="bundle",
+        )(*[held(value) for value in (momentum, face_even, acc_e1, acc_o1, acc_o2)])
+        bundle = lax.ppermute(bundle, "cross", side_pairs(cols, 0))
+        momentum, send_e1, send_o1, send_o2 = pl.pallas_call(
+            exchange_kernel,
+            out_shape=[near(3, NODES, NODES, lanes)]
+            + [near(4, NODES, lanes)] * 2
+            + [near(NODES, capacity)],
+            in_specs=[vmem] * 2,
+            out_specs=[vmem] * 4,
+            name="cross_faces",
+        )(held(momentum), held(bundle))
+    else:
+        swap = 0
+        face_even = lax.ppermute(face_even, "cross", side_pairs(cols, 0))
+        face_odd = lax.ppermute(face_odd[0], "cross", side_pairs(cols, 1))
+        momentum, send_e1, send_o1 = pl.pallas_call(
+            middle_kernel,
+            out_shape=[near(3, NODES, NODES, lanes)] + [near(4, NODES, lanes)] * 2,
+            in_specs=[vmem] * 5,
+            out_specs=[vmem] * 3,
+            name="cross_faces",
+        )(*[held(value) for value in (momentum, face_even, face_odd, acc_e1, acc_o1)])
+        send_o2 = acc_o2
+    got_o2 = returned(send_o2, 3, swap)
+    got_e1 = returned(send_e1, 0, swap)
+    got_o1 = returned(send_o1, 1, swap)
+    pressure, momentum, accel = pl.pallas_call(
+        lambda *refs: last_kernel(slabs, reach, *refs),
+        out_shape=[f32(NODES, NODES, lanes), f32(3, NODES, NODES, lanes), f32(3 * reach, 1, capacity)],
+        in_specs=[vmem] * 7,
         out_specs=[vmem] * 3,
-        name="cross_faces",
-    )(*[held(value) for value in (momentum, face_even, face_odd, acc_e1, acc_o1)])
-    got_e1, got_o1 = [
-        lax.ppermute(value, whole, neighbours(slabs, cols, *route))
-        for value, route in zip((send_e1, send_o1), ROUTES[:2])
-    ]
-    momentum, accel = pl.pallas_call(
-        lambda *refs: last_kernel(slabs, reach, *refs),
-        out_shape=[f32(3, NODES, NODES, lanes), f32(3 * reach, 1, capacity)],
-        in_specs=[vmem] * 6,
-        out_specs=[vmem] * 2,
         name="stream_faces",
-    )(*[held(value) for value in (momentum, got_e1, got_o1, acc_own, got_e2, got_o2)])
+    )(*[held(value) for value in (pressure, momentum, got_e1, got_o1, acc_own, got_e2, got_o2)])
     return (pressure, momentum, accel.reshape(1, 1, reach, 3, capacity))
 
 

time: 39.9 us -> 40.2 us (level)
  local copies, waits for them, and re-layouts: 0.02 us -> 0.68 us
  waiting for transfers between devices: 19.3 us -> 18.8 us
    ppermute x8 -> x4, waiting for transfers between devices: 12.8 us -> 8.33 us  [step(): lax.ppermute(value, whole, neighbours(slabs, cols, *route))]
    ppermute x1 -> x5, waiting for transfers between devices: 1.18 us -> 5.15 us  [the longest x4 3.93 us: returned(): return lax.ppermute(value, whole, pairs)]
    ppermute x8 -> x4, starting transfers between devices: 7.15 us -> 3.6 us  [step(): lax.ppermute(value, whole, neighbours(slabs, cols, *route))]
    ppermute x1 -> x5, starting transfers between devices: 0.01 us -> 3.34 us  [the longest x4 3.27 us: returned(): return lax.ppermute(value, whole, pairs)]
    unnamed x10, local copies, waits for them, and re-layouts: 0.02 us -> 0.68 us
where the time goes in v1:
time: 40.2 us; the launch traced here: 39.5 us
  waiting for transfers between devices  18.8 us (47%)
  starting transfers between devices  15.1 us (38%)
  Pallas kernels  4.18 us (10%)
  between operations  0.78 us (2%)
  local copies, waits for them, and re-layouts  0.68 us (2%)
    ppermute x4, waiting for transfers between devices, step(): lax.ppermute(value, whole, neighbours(slabs, cols, *route))  8.33 us
    ppermute x4, waiting for transfers between devices, returned(): return lax.ppermute(value, whole, pairs)  3.93 us
    ppermute x4, starting transfers between devices, step(): lax.ppermute(value, whole, neighbours(slabs, cols, *route))  3.6 us
    ppermute x4, starting transfers between devices, returned(): return lax.ppermute(value, whole, pairs)  3.27 us
    ppermute x2, starting transfers between devices, step(): lax.ppermute(value, whole, neighbours(slabs, cols, DEPTH, odd, 1))  2.94 us
    pallas_call x1, Pallas kernels, step(): pl.pallas_call(lambda *refs: main_kernel(slabs, cols, *refs), out_shape=[...  2.45 us
    ppermute x1, waiting for transfers between devices, step(): lax.ppermute(gathered, whole, swapped_bit(slabs, cols, 2))  2.04 us
    ppermute x1, starting transfers between devices, step(): lax.ppermute(gathered, whole, swapped_bit(slabs, cols, 2))  1.87 us
  transfers between devices with their start and end apart: 17, of which 10 were waited for; matrix products, arithmetic and copies ran while one was open for 0% of the time, Pallas kernels for 2%

profile of v1, /device:TPU:8, one launch (start us, length us, event | category | flops | bytes accessed | tf_op | source)
XLA Modules:
  0.0 39.5 jit_solution(18275849013418912896)
XLA Ops:
  0.6 1.0 %collective-permute-start = (f32[8,8,128]{2,1,0:T(8,128)}, f32[8,8,128]{2,1,0:T(8,128)S(1)}, u32[]{:S(2)}, u32[]{:S(2)}) collective-permute-start(f32[8,8,128]{2,1,0:T(8,128)} %refs_0_.3), channel_id=1, source_target_pairs={{0,3},{1,2},{2,1},{3,0},{4,7},{5,6},{6,5},{7,4},{8,11},{9,10},{10,... | collective-permute-start | bytes 98312 | tf_op jit(solution)/shard_map/ppermute | solution.py:673
  1.6 0.8 %collective-permute-start.1 = (f32[1,1,16]{2,1,0:T(1,128)}, f32[1,1,16]{2,1,0:T(1,128)S(1)}, u32[]{:S(2)}, u32[]{:S(2)}) collective-permute-start(f32[1,1,16]{2,1,0:T(1,128)} %refs_1_.2), channel_id=1, source_target_pairs={{0,3},{1,2},{2,1},{3,0},{4,7},{5,6},{6,5},{7,4},{8,11},{9,10},{10,... | collective-permute-start | bytes 200 | tf_op jit(solution)/shard_map/ppermute | solution.py:674
  2.4 0.8 %pack.1 = (f32[9,8,128]{2,1,0:T(8,128)S(1)}, f32[2,8,128]{2,1,0:T(8,128)S(1)}, f32[2,8,128]{2,1,0:T(8,128)S(1)}, f32[2,8,128]{2,1,0:T(8,128)S(1)}, f32[2,8,128]{2,1,0:T(8,128)S(1)}, /*index=5*/f32[2,8,128]{2,1,0:T(8,128)S(1)}) custom-call(f32[8,8,128]{2,1,0:T(8,128)} %refs_0_.3, f32[1,1,16]{2,1,0:T(1,128)} %refs_1_.2, s32[5,1,128]{2,1,0:T(1,128)} %bitcast.8, ...), custom_call_target="tpu_custom_call" | custom-call | tf_op jit(solution)/shard_map/pack/pallas_call | solution.py:651
  3.3 1.5 %collective-permute-done.1.from_metric = f32[1,1,16]{2,1,0:T(1,128)S(1)} collective-permute-done((f32[1,1,16]{2,1,0:T(1,128)}, f32[1,1,16]{2,1,0:T(1,128)S(1)}, u32[]{:S(2)}, u32[]{:S(2)}) %collective-permute-start.1) | collective-permute-done | bytes 96 | tf_op jit(solution)/shard_map/ppermute | solution.py:674
  4.8 0.0 collective-permute-done.from_source
  4.8 1.9 %collective-permute-start.2 = (f32[2,9,8,128]{3,2,1,0:T(8,128)S(1)}, f32[2,9,8,128]{3,2,1,0:T(8,128)S(1)}, u32[]{:S(2)}, u32[]{:S(2)}) collective-permute-start(f32[2,9,8,128]{3,2,1,0:T(8,128)S(1)} %near_pair.1), channel_id=1, source_target_pairs={{0,5},{1,4},{2,7},{3,6},{4,1},{5,0},{6,3},{7,2},{8,13},{9,12},{10,... | collective-permute-start | bytes 221192 | tf_op jit(solution)/shard_map/ppermute | solution.py:683
  6.6 2.0 %collective-permute-done.2 = f32[2,9,8,128]{3,2,1,0:T(8,128)S(1)} collective-permute-done((f32[2,9,8,128]{3,2,1,0:T(8,128)S(1)}, f32[2,9,8,128]{3,2,1,0:T(8,128)S(1)}, u32[]{:S(2)}, u32[]{:S(2)}) %collective-permute-start.2) | collective-permute-done | bytes 73760 | tf_op jit(solution)/shard_map/ppermute | solution.py:683
  8.7 0.0 copy-start.2
  8.7 0.0 copy-start.3
  8.7 0.0 copy-start
  8.7 0.0 copy-start.1
  8.8 0.7 %collective-permute-start.3 = (f32[26,8,128]{2,1,0:T(8,128)S(1)}, f32[26,8,128]{2,1,0:T(8,128)S(1)}, u32[]{:S(2)}, u32[]{:S(2)}) collective-permute-start(f32[26,8,128]{2,1,0:T(8,128)S(1)} %get-tuple-element.31), channel_id=1, source_target_pairs={{0,9},{1,8},{2,11},{3,10},{4,13},{5,12},{6,15},{7,14},{8,1},{9,0},... | collective-permute-start | bytes 319496 | tf_op jit(solution)/shard_map/ppermute | solution.py:693
  9.5 2.2 %collective-permute-start.4 = (f32[26,8,128]{2,1,0:T(8,128)S(1)}, f32[26,8,128]{2,1,0:T(8,128)S(1)}, u32[]{:S(2)}, u32[]{:S(2)}) collective-permute-start(f32[26,8,128]{2,1,0:T(8,128)S(1)} %get-tuple-element.32), channel_id=1, source_target_pairs={{0,1},{1,0},{2,3},{3,2},{4,5},{5,4},{6,7},{7,6},{8,17},{9,16},{10,... | collective-permute-start | bytes 319496 | tf_op jit(solution)/shard_map/ppermute | solution.py:693
  11.7 0.6 %collective-permute-start.5 = (f32[4,9,8,128]{3,2,1,0:T(8,128)S(1)}, f32[4,9,8,128]{3,2,1,0:T(8,128)S(1)}, u32[]{:S(2)}, u32[]{:S(2)}) collective-permute-start(f32[4,9,8,128]{3,2,1,0:T(8,128)S(1)} %pad_maximum_fusion.gathered.refs_4_), channel_id=1, source_target_pairs={{0,1},{1,0},{2,3},{3,2},{4,5},{5,4},{6,7},{7,6},{8,9},{9,8},{10,11... | collective-permute-start | bytes 442376 | tf_op jit(solution)/shard_map/ppermute | solution.py:700
  12.3 1.0 %collective-permute-done.3.refs_5_ = f32[26,8,128]{2,1,0:T(8,128)S(1)} collective-permute-done((f32[26,8,128]{2,1,0:T(8,128)S(1)}, f32[26,8,128]{2,1,0:T(8,128)S(1)}, u32[]{:S(2)}, u32[]{:S(2)}) %collective-permute-start.3) | collective-permute-done | bytes 106528 | tf_op jit(solution)/shard_map/ppermute | solution.py:693
  13.3 0.9 %collective-permute-start.6 = (f32[26,8,128]{2,1,0:T(8,128)S(1)}, f32[26,8,128]{2,1,0:T(8,128)S(1)}, u32[]{:S(2)}, u32[]{:S(2)}) collective-permute-start(f32[26,8,128]{2,1,0:T(8,128)S(1)} %collective-permute-done.3.refs_5_), channel_id=1, source_target_pairs={{0,1},{1,0},{2,3},{3,2},{4,5},{5,4},{6,7},{7,6},{8,9},{9,8},{10,11... | collective-permute-start | bytes 319496 | tf_op jit(solution)/shard_map/ppermute | solution.py:700
  14.2 0.8 %collective-permute-done.4.refs_6_ = f32[26,8,128]{2,1,0:T(8,128)S(1)} collective-permute-done((f32[26,8,128]{2,1,0:T(8,128)S(1)}, f32[26,8,128]{2,1,0:T(8,128)S(1)}, u32[]{:S(2)}, u32[]{:S(2)}) %collective-permute-start.4) | collective-permute-done | bytes 106528 | tf_op jit(solution)/shard_map/ppermute | solution.py:693
  15.0 0.0 collective-permute-start.7
  15.0 1.9 %collective-permute-start.8 = (f32[2,8,128]{2,1,0:T(8,128)S(1)}, f32[2,8,128]{2,1,0:T(8,128)S(1)}, u32[]{:S(2)}, u32[]{:S(2)}) collective-permute-start(f32[2,8,128]{2,1,0:T(8,128)S(1)} %get-tuple-element.34), channel_id=1, source_target_pairs={{0,2},{1,3},{2,0},{3,1},{4,6},{5,7},{6,4},{7,5},{8,10},{9,11},{10,... | collective-permute-start | bytes 24584 | tf_op jit(solution)/shard_map/ppermute | solution.py:670
  17.0 0.1 collective-permute-start.9
  17.1 1.6 %collective-permute-done.8.refs_2_.refs_12_ = f32[2,8,128]{2,1,0:T(8,128)S(1)} collective-permute-done((f32[2,8,128]{2,1,0:T(8,128)S(1)}, f32[2,8,128]{2,1,0:T(8,128)S(1)}, u32[]{:S(2)}, u32[]{:S(2)}) %collective-permute-start.8) | collective-permute-done | bytes 8224 | tf_op jit(solution)/shard_map/ppermute | solution.py:670
  18.7 1.6 %collective-permute-start.10 = (f32[2,8,128]{2,1,0:T(8,128)S(1)}, f32[2,8,128]{2,1,0:T(8,128)S(1)}, u32[]{:S(2)}, u32[]{:S(2)}) collective-permute-start(f32[2,8,128]{2,1,0:T(8,128)S(1)} %get-tuple-element.36), channel_id=1, source_target_pairs={{0,4},{1,5},{2,6},{3,7},{4,0},{5,1},{6,2},{7,3},{8,12},{9,13},{10,... | collective-permute-start | bytes 24584 | tf_op jit(solution)/shard_map/ppermute | solution.py:670
  20.3 2.2 %collective-permute-done.9.refs_3_.refs_13_ = f32[2,8,128]{2,1,0:T(8,128)S(1)} collective-permute-done((f32[2,8,128]{2,1,0:T(8,128)S(1)}, f32[2,8,128]{2,1,0:T(8,128)S(1)}, u32[]{:S(2)}, u32[]{:S(2)}) %collective-permute-start.9) | collective-permute-done | bytes 8224 | tf_op jit(solution)/shard_map/ppermute | solution.py:670
  22.4 0.0 collective-permute-start.11
  22.4 0.0 collective-permute-done.10.refs_4_.refs_14_
  22.4 4.5 %collective-permute-done.11.refs_5_.refs_15_ = f32[2,8,128]{2,1,0:T(8,128)S(1)} collective-permute-done((f32[2,8,128]{2,1,0:T(8,128)S(1)}, f32[2,8,128]{2,1,0:T(8,128)S(1)}, u32[]{:S(2)}, u32[]{:S(2)}) %collective-permute-start.11) | collective-permute-done | bytes 8224 | tf_op jit(solution)/shard_map/ppermute | solution.py:670
  27.0 0.0 copy-done
  27.0 0.0 copy-start.4
  27.0 0.1 bases.1
  27.1 0.0 collective-permute-done.5.refs_7_
  27.1 0.0 collective-permute-done.6.refs_8_
  27.1 0.0 collective-permute-done.7.refs_9_
  27.1 0.0 copy-done.2
  27.1 0.0 copy-done.3
  27.2 0.0 copy-done.1
  27.2 0.7 %copy-done.4 = bf16[256,128]{1,0:T(8,128)(2,1)S(1)} copy-done((bf16[256,128]{1,0:T(8,128)(2,1)S(1)}, bf16[256,128]{1,0:T(8,128)(2,1)}, u32[]{:S(2)}) %copy-start.4) | copy-done | bytes 65560
  27.8 2.4 %sweeps_and_droplets.1 = (f32[8,8,128]{2,1,0:T(8,128)S(1)}, f32[3,8,8,128]{3,2,1,0:T(8,128)S(1)}, f32[3,8,128]{2,1,0:T(8,128)S(1)}, f32[8,128]{1,0:T(8,128)S(1)}...) custom-call(f32[33,8,128]{2,1,0:T(8,128)S(1)} %copy-done, ...), custom_call_target="tpu_custom_call" | custom-call | tf_op jit(solution)/shard_map/sweeps_and_droplets/pallas_call | solution.py:718
  30.3 0.1 collective-permute-start.12
  30.4 1.2 %collective-permute-done.12.got = f32[12,8,128]{2,1,0:T(8,128)S(1)} collective-permute-done((f32[12,8,128]{2,1,0:T(8,128)S(1)}, f32[12,8,128]{2,1,0:T(8,128)S(1)}, u32[]{:S(2)}, u32[]{:S(2)}) %collective-permute-start.12) | collective-permute-done | bytes 49184 | tf_op jit(solution)/shard_map/ppermute | solution.py:764
  31.7 0.1 collective-permute-start.13
  31.7 1.2 %collective-permute-start.14 = (f32[4,8,128]{2,1,0:T(8,128)S(1)}, f32[4,8,128]{2,1,0:T(8,128)S(1)}, u32[]{:S(2)}, u32[]{:S(2)}) collective-permute-start(f32[4,8,128]{2,1,0:T(8,128)S(1)} %get-tuple-element.50), channel_id=1, source_target_pairs={{0,1},{1,0},{2,5},{3,4},{4,3},{5,2},{6,9},{7,8},{8,7},{9,6},{10,13... | collective-permute-start | bytes 49160 | tf_op jit(solution)/shard_map/ppermute | solution.py:752
  32.9 2.0 %collective-permute-start.15 = (f32[8,128]{1,0:T(8,128)S(1)}, f32[8,128]{1,0:T(8,128)S(1)}, u32[]{:S(2)}, u32[]{:S(2)}) collective-permute-start(f32[8,128]{1,0:T(8,128)S(1)} %get-tuple-element.52), channel_id=1, source_target_pairs={{0,4},{1,5},{2,6},{3,7},{4,0},{5,1},{6,2},{7,3},{8,12},{9,13},{10,... | collective-permute-start | bytes 12296 | tf_op jit(solution)/shard_map/ppermute | solution.py:752
  34.9 0.0 collective-permute-start.16
  34.9 1.6 %collective-permute-done.15.refs_5_ = f32[8,128]{1,0:T(8,128)S(1)} collective-permute-done((f32[8,128]{1,0:T(8,128)S(1)}, f32[8,128]{1,0:T(8,128)S(1)}, u32[]{:S(2)}, u32[]{:S(2)}) %collective-permute-start.15) | collective-permute-done | bytes 4128 | tf_op jit(solution)/shard_map/ppermute | solution.py:752
  36.5 2.3 %collective-permute-done.16.refs_6_ = f32[8,128]{1,0:T(8,128)S(1)} collective-permute-done((f32[8,128]{1,0:T(8,128)S(1)}, f32[8,128]{1,0:T(8,128)S(1)}, u32[]{:S(2)}, u32[]{:S(2)}) %collective-permute-start.16) | collective-permute-done | bytes 4128 | tf_op jit(solution)/shard_map/ppermute | solution.py:752
  38.9 0.0 collective-permute-done.13.refs_2_
  38.9 0.0 collective-permute-done.14.refs_3_
  38.9 0.7 %stream_faces.1 = (f32[8,8,128]{2,1,0:T(8,128)}, f32[3,8,8,128]{3,2,1,0:T(8,128)}, f32[15,1,128]{2,1,0:T(1,128)}) custom-call(f32[8,8,128]{2,1,0:T(8,128)S(1)} %get-tuple-element.42.refs_0_, f32[3,8,8,128]{3,2,1,0:T(8,128)S(1)} %get-tuple-element.48.refs_1_, f32[4,8,128]{2,1,0:T(8,128)S(1)} %collective-permute-done.13.refs_2_, ...), custom_call_target="tpu_custom_call" | custom-call | tf_op jit(solution)/shard_map/stream_faces/pallas_call | solution.py:789
  (5 shorter events, 0.1 us)
Async XLA Ops:
  0.6 4.1 %collective-permute-start = (f32[8,8,128]{2,1,0:T(8,128)}, f32[8,8,128]{2,1,0:T(8,128)S(1)}, u32[]{:S(2)}, u32[]{:S(2)}) collective-permute-start(f32[8,8,128]{2,1,0:T(8,128)} %refs_0_.3), channel_id=1, source_target_pairs={{0,3},{1,2},{2,1},{3,0},{4,7},{5,6},{6,5},{7,4},{8,11},{9,10},{10,... | collective-permute-start | bytes 98312 | tf_op jit(solution)/shard_map/ppermute | solution.py:673
  1.6 3.1 %collective-permute-start.1 = (f32[1,1,16]{2,1,0:T(1,128)}, f32[1,1,16]{2,1,0:T(1,128)S(1)}, u32[]{:S(2)}, u32[]{:S(2)}) collective-permute-start(f32[1,1,16]{2,1,0:T(1,128)} %refs_1_.2), channel_id=1, source_target_pairs={{0,3},{1,2},{2,1},{3,0},{4,7},{5,6},{6,5},{7,4},{8,11},{9,10},{10,... | collective-permute-start | bytes 200 | tf_op jit(solution)/shard_map/ppermute | solution.py:674
  4.8 3.9 %collective-permute-start.2 = (f32[2,9,8,128]{3,2,1,0:T(8,128)S(1)}, f32[2,9,8,128]{3,2,1,0:T(8,128)S(1)}, u32[]{:S(2)}, u32[]{:S(2)}) collective-permute-start(f32[2,9,8,128]{3,2,1,0:T(8,128)S(1)} %near_pair.1), channel_id=1, source_target_pairs={{0,5},{1,4},{2,7},{3,6},{4,1},{5,0},{6,3},{7,2},{8,13},{9,12},{10,... | collective-permute-start | bytes 221192 | tf_op jit(solution)/shard_map/ppermute | solution.py:683
  8.7 18.5 %copy-start.2 = (bf16[256,256]{1,0:T(8,128)(2,1)S(1)}, bf16[256,256]{1,0:T(8,128)(2,1)}, u32[]{:S(2)}) copy-start(bf16[256,256]{1,0:T(8,128)(2,1)} %constant.9.clone.refs_1_) | copy-start | bytes 393220
  8.7 18.5 %copy-start.3 = (f32[3,8,8,128]{3,2,1,0:T(8,128)S(1)}, f32[3,8,8,128]{3,2,1,0:T(8,128)}, u32[]{:S(2)}) copy-start(f32[3,8,8,128]{3,2,1,0:T(8,128)} %refs_10_.1) | copy-start | bytes 294916
  8.7 18.3 %copy-start = (f32[33,8,128]{2,1,0:T(8,128)S(1)}, f32[33,8,128]{2,1,0:T(8,128)}, u32[]{:S(2)}) copy-start(f32[33,8,128]{2,1,0:T(8,128)} %constant.8.clone.refs_0_) | copy-start | bytes 405508
  8.7 18.4 %copy-start.1 = (bf16[256,256]{1,0:T(8,128)(2,1)S(1)}, bf16[256,256]{1,0:T(8,128)(2,1)}, u32[]{:S(2)}) copy-start(bf16[256,256]{1,0:T(8,128)(2,1)} %constant.10.clone.refs_2_) | copy-start | bytes 393220
  8.8 4.5 %collective-permute-start.3 = (f32[26,8,128]{2,1,0:T(8,128)S(1)}, f32[26,8,128]{2,1,0:T(8,128)S(1)}, u32[]{:S(2)}, u32[]{:S(2)}) collective-permute-start(f32[26,8,128]{2,1,0:T(8,128)S(1)} %get-tuple-element.31), channel_id=1, source_target_pairs={{0,9},{1,8},{2,11},{3,10},{4,13},{5,12},{6,15},{7,14},{8,1},{9,0},... | collective-permute-start | bytes 319496 | tf_op jit(solution)/shard_map/ppermute | solution.py:693
  9.5 5.5 %collective-permute-start.4 = (f32[26,8,128]{2,1,0:T(8,128)S(1)}, f32[26,8,128]{2,1,0:T(8,128)S(1)}, u32[]{:S(2)}, u32[]{:S(2)}) collective-permute-start(f32[26,8,128]{2,1,0:T(8,128)S(1)} %get-tuple-element.32), channel_id=1, source_target_pairs={{0,1},{1,0},{2,3},{3,2},{4,5},{5,4},{6,7},{7,6},{8,17},{9,16},{10,... | collective-permute-start | bytes 319496 | tf_op jit(solution)/shard_map/ppermute | solution.py:693
  11.7 15.4 %collective-permute-start.5 = (f32[4,9,8,128]{3,2,1,0:T(8,128)S(1)}, f32[4,9,8,128]{3,2,1,0:T(8,128)S(1)}, u32[]{:S(2)}, u32[]{:S(2)}) collective-permute-start(f32[4,9,8,128]{3,2,1,0:T(8,128)S(1)} %pad_maximum_fusion.gathered.refs_4_), channel_id=1, source_target_pairs={{0,1},{1,0},{2,3},{3,2},{4,5},{5,4},{6,7},{7,6},{8,9},{9,8},{10,11... | collective-permute-start | bytes 442376 | tf_op jit(solution)/shard_map/ppermute | solution.py:700
  13.3 13.8 %collective-permute-start.6 = (f32[26,8,128]{2,1,0:T(8,128)S(1)}, f32[26,8,128]{2,1,0:T(8,128)S(1)}, u32[]{:S(2)}, u32[]{:S(2)}) collective-permute-start(f32[26,8,128]{2,1,0:T(8,128)S(1)} %collective-permute-done.3.refs_5_), channel_id=1, source_target_pairs={{0,1},{1,0},{2,3},{3,2},{4,5},{5,4},{6,7},{7,6},{8,9},{9,8},{10,11... | collective-permute-start | bytes 319496 | tf_op jit(solution)/shard_map/ppermute | solution.py:700
  15.0 12.1 %collective-permute-start.7 = (f32[26,8,128]{2,1,0:T(8,128)S(1)}, f32[26,8,128]{2,1,0:T(8,128)S(1)}, u32[]{:S(2)}, u32[]{:S(2)}) collective-permute-start(f32[26,8,128]{2,1,0:T(8,128)S(1)} %collective-permute-done.4.refs_6_), channel_id=1, source_target_pairs={{0,1},{1,0},{2,3},{3,2},{4,5},{5,4},{6,7},{7,6},{8,9},{9,8},{10,11... | collective-permute-start | bytes 319496 | tf_op jit(solution)/shard_map/ppermute | solution.py:700
  15.0 3.7 %collective-permute-start.8 = (f32[2,8,128]{2,1,0:T(8,128)S(1)}, f32[2,8,128]{2,1,0:T(8,128)S(1)}, u32[]{:S(2)}, u32[]{:S(2)}) collective-permute-start(f32[2,8,128]{2,1,0:T(8,128)S(1)} %get-tuple-element.34), channel_id=1, source_target_pairs={{0,2},{1,3},{2,0},{3,1},{4,6},{5,7},{6,4},{7,5},{8,10},{9,11},{10,... | collective-permute-start | bytes 24584 | tf_op jit(solution)/shard_map/ppermute | solution.py:670
  17.0 5.5 %collective-permute-start.9 = (f32[2,8,128]{2,1,0:T(8,128)S(1)}, f32[2,8,128]{2,1,0:T(8,128)S(1)}, u32[]{:S(2)}, u32[]{:S(2)}) collective-permute-start(f32[2,8,128]{2,1,0:T(8,128)S(1)} %get-tuple-element.35), channel_id=1, source_target_pairs={{0,1},{1,0},{2,4},{3,5},{4,2},{5,3},{6,8},{7,9},{8,6},{9,7},{10,12... | collective-permute-start | bytes 24584 | tf_op jit(solution)/shard_map/ppermute | solution.py:670
  18.7 3.7 %collective-permute-start.10 = (f32[2,8,128]{2,1,0:T(8,128)S(1)}, f32[2,8,128]{2,1,0:T(8,128)S(1)}, u32[]{:S(2)}, u32[]{:S(2)}) collective-permute-start(f32[2,8,128]{2,1,0:T(8,128)S(1)} %get-tuple-element.36), channel_id=1, source_target_pairs={{0,4},{1,5},{2,6},{3,7},{4,0},{5,1},{6,2},{7,3},{8,12},{9,13},{10,... | collective-permute-start | bytes 24584 | tf_op jit(solution)/shard_map/ppermute | solution.py:670
  22.4 4.5 %collective-permute-start.11 = (f32[2,8,128]{2,1,0:T(8,128)S(1)}, f32[2,8,128]{2,1,0:T(8,128)S(1)}, u32[]{:S(2)}, u32[]{:S(2)}) collective-permute-start(f32[2,8,128]{2,1,0:T(8,128)S(1)} %get-tuple-element.37), channel_id=1, source_target_pairs={{0,1},{1,0},{2,3},{3,2},{4,8},{5,9},{6,10},{7,11},{8,4},{9,5},{10,... | collective-permute-start | bytes 24584 | tf_op jit(solution)/shard_map/ppermute | solution.py:670
  27.0 0.8 %copy-start.4 = (bf16[256,128]{1,0:T(8,128)(2,1)S(1)}, bf16[256,128]{1,0:T(8,128)(2,1)}, u32[]{:S(2)}) copy-start(bf16[256,128]{1,0:T(8,128)(2,1)} %constant.11.clone.refs_3_) | copy-start | bytes 196612
  30.3 1.3 %collective-permute-start.12 = (f32[12,8,128]{2,1,0:T(8,128)S(1)}, f32[12,8,128]{2,1,0:T(8,128)S(1)}, u32[]{:S(2)}, u32[]{:S(2)}) collective-permute-start(f32[12,8,128]{2,1,0:T(8,128)S(1)} %bundle.1), channel_id=1, source_target_pairs={{0,1},{1,0},{2,3},{3,2},{4,5},{5,4},{6,7},{7,6},{8,9},{9,8},{10,11... | collective-permute-start | bytes 147464 | tf_op jit(solution)/shard_map/ppermute | solution.py:764
  31.7 7.2 %collective-permute-start.13 = (f32[4,8,128]{2,1,0:T(8,128)S(1)}, f32[4,8,128]{2,1,0:T(8,128)S(1)}, u32[]{:S(2)}, u32[]{:S(2)}) collective-permute-start(f32[4,8,128]{2,1,0:T(8,128)S(1)} %get-tuple-element.49), channel_id=1, source_target_pairs={{0,3},{1,2},{2,1},{3,0},{4,7},{5,6},{6,5},{7,4},{8,11},{9,10},{10,... | collective-permute-start | bytes 49160 | tf_op jit(solution)/shard_map/ppermute | solution.py:752
  31.7 7.1 %collective-permute-start.14 = (f32[4,8,128]{2,1,0:T(8,128)S(1)}, f32[4,8,128]{2,1,0:T(8,128)S(1)}, u32[]{:S(2)}, u32[]{:S(2)}) collective-permute-start(f32[4,8,128]{2,1,0:T(8,128)S(1)} %get-tuple-element.50), channel_id=1, source_target_pairs={{0,1},{1,0},{2,5},{3,4},{4,3},{5,2},{6,9},{7,8},{8,7},{9,6},{10,13... | collective-permute-start | bytes 49160 | tf_op jit(solution)/shard_map/ppermute | solution.py:752
  32.9 3.6 %collective-permute-start.15 = (f32[8,128]{1,0:T(8,128)S(1)}, f32[8,128]{1,0:T(8,128)S(1)}, u32[]{:S(2)}, u32[]{:S(2)}) collective-permute-start(f32[8,128]{1,0:T(8,128)S(1)} %get-tuple-element.52), channel_id=1, source_target_pairs={{0,4},{1,5},{2,6},{3,7},{4,0},{5,1},{6,2},{7,3},{8,12},{9,13},{10,... | collective-permute-start | bytes 12296 | tf_op jit(solution)/shard_map/ppermute | solution.py:752
  34.9 3.9 %collective-permute-start.16 = (f32[8,128]{1,0:T(8,128)S(1)}, f32[8,128]{1,0:T(8,128)S(1)}, u32[]{:S(2)}, u32[]{:S(2)}) collective-permute-start(f32[8,128]{1,0:T(8,128)S(1)} %get-tuple-element.53), channel_id=1, source_target_pairs={{0,1},{1,0},{2,3},{3,2},{4,9},{5,8},{6,11},{7,10},{8,5},{9,4},{10,... | collective-permute-start | bytes 12296 | tf_op jit(solution)/shard_map/ppermute | solution.py:752

commit v2 on v1

--- a/solution.py
+++ b/solution.py
@@ -306,7 +306,7 @@
 
 
 def basis_kernel(slabs, tiles, own, *rest):
-    routed, (high, low, cells, live) = rest[:4], rest[4:]
+    routed, (picks, cells, live) = rest[:4], rest[4:]
     position = lax.axis_index("stream")
     lanes, capacity = tiles.shape[-1], own.shape[-1]
     opened = [None] + [route_open(position, route, slabs) for route in ROUTES]
@@ -320,7 +320,7 @@
             [jnp.where(ids == float(e + 1), basis[2], 0.0) for e in range(lanes // NODES)], 0
         )
         place = slice(g * capacity, (g + 1) * capacity)
-        high[:, place], low[:, place] = split_value(pick)
+        picks[0:lanes, place], picks[lanes : 2 * lanes, place] = split_value(pick)
         for i in range(NODES):
             cells[g, i] = basis[1] * basis[0][i : i + 1, :]
 
@@ -330,9 +330,9 @@
     pieces = refs[4 : 4 + 3 * cols]
     base_velocity, own = refs[4 + 3 * cols : 6 + 3 * cols]
     routed = refs[6 + 3 * cols : 10 + 3 * cols]
-    picks_high, picks_low, cells_ref, live = refs[10 + 3 * cols : 14 + 3 * cols]
+    picks, cells_ref, live = refs[10 + 3 * cols : 13 + 3 * cols]
     (pressure, momentum, face_even, acc_own, acc_e1, acc_o1, acc_e2, acc_o2,
-     *face_odd, loads, scales, resid, update, inv, work, spans, layers) = refs[14 + 3 * cols :]
+     *face_odd, loads, scales, resid, update, inv, work, spans, layers) = refs[13 + 3 * cols :]
     lanes = tiles.shape[-1]
     position = lax.axis_index("stream")
     column = lax.axis_index("cross")
@@ -503,13 +503,16 @@
         velocity.append(base_velocity[2, i] - scale * grad_z[i])
     velocity = jnp.concatenate(velocity, 0)
 
-    pick_high, pick_low = picks_high[...], picks_low[...]
-    vel_high, vel_low = split_value(velocity)
+    count = 3 * NODES * NODES
+    high, low = split_value(velocity)
     partial = jnp.dot(
-        jnp.concatenate([vel_high, vel_low, vel_high], 1),
-        jnp.concatenate([pick_high, pick_high, pick_low], 0),
+        jnp.concatenate(
+            [jnp.concatenate([high, high], 1), jnp.concatenate([low, low], 1)], 0
+        ),
+        picks[...],
         preferred_element_type=F32,
     )
+    partial = partial[:count] + partial[count:]
     capacity = own.shape[-1]
     spread = []
     for g, group in enumerate((own,) + tuple(routed)):
@@ -531,13 +534,14 @@
         (acc_own, acc_e1, acc_o1, acc_e2, acc_o2)[g][...] = jnp.concatenate(accel_rows, 0)
         spread.append(jnp.concatenate(parts, 0))
     spread = jnp.concatenate(spread, 1)
-    spread_high, spread_low = split_value(spread)
     added = lax.dot_general(
-        jnp.concatenate([spread_high, spread_low, spread_high], 1),
-        jnp.concatenate([pick_high, pick_high, pick_low], 1),
+        jnp.concatenate(split_value(spread), 0),
+        picks[...],
         (((1,), (1,)), ((), ())),
         preferred_element_type=F32,
     )
+    added = added[:count] + added[count:]
+    added = added[:, :lanes] + added[:, lanes:]
     added = z_assembled(added.reshape(3, NODES, NODES, lanes), tiles)
     momentum[...] = added
     low_row = added[:, :, 0, :]
@@ -709,10 +713,10 @@
     slots = 5 * capacity
     bases = pl.pallas_call(
         lambda *refs: basis_kernel(slabs, *refs),
-        out_shape=[pltpu.VMEM((lanes, slots), BF16)] * 2
+        out_shape=[pltpu.VMEM((2 * lanes, slots), BF16)]
         + [near(5, NODES, NODES, capacity), near(5, NODES, capacity)],
         in_specs=[vmem] * 6,
-        out_specs=[vmem] * 4,
+        out_specs=[vmem] * 3,
         name="bases",
     )(held(tiles), held(own), *[held(value) for value in routed])
     pressure, momentum, face_even, *accels = pl.pallas_call(
@@ -721,7 +725,7 @@
         + [near(3, NODES, lanes)]
         + [near(NODES, capacity)] * 5
         + [near(3, NODES, lanes)] * (cols > 2),
-        in_specs=[vmem] * (14 + 3 * cols),
+        in_specs=[vmem] * (13 + 3 * cols),
         out_specs=[vmem] * (8 + (cols > 2)),
         scratch_shapes=[
             pltpu.VMEM((4 * DEPTH - 1,) + field, F32),

time: 40.2 us -> 39.4 us (0.980)
  local copies, waits for them, and re-layouts: 0.68 us -> 0.03 us
    unnamed x10, local copies, waits for them, and re-layouts: 0.68 us -> 0.03 us
where the time goes in v2:
time: 39.4 us; the launch traced here: 38.7 us
  waiting for transfers between devices  18.8 us (48%)
  starting transfers between devices  15.1 us (38%)
  Pallas kernels  4.01 us (10%)
  between operations  0.79 us (2%)
    ppermute x4, waiting for transfers between devices, step(): lax.ppermute(value, whole, neighbours(slabs, cols, *route))  8.33 us
    ppermute x4, waiting for transfers between devices, returned(): return lax.ppermute(value, whole, pairs)  3.93 us
    ppermute x4, starting transfers between devices, step(): lax.ppermute(value, whole, neighbours(slabs, cols, *route))  3.6 us
    ppermute x4, starting transfers between devices, returned(): return lax.ppermute(value, whole, pairs)  3.27 us
    ppermute x2, starting transfers between devices, step(): lax.ppermute(value, whole, neighbours(slabs, cols, DEPTH, odd, 1))  2.94 us
    pallas_call x1, Pallas kernels, step(): pl.pallas_call(lambda *refs: main_kernel(slabs, cols, *refs), out_shape=[...  2.28 us
    ppermute x1, waiting for transfers between devices, step(): lax.ppermute(gathered, whole, swapped_bit(slabs, cols, 2))  2.04 us
    ppermute x1, starting transfers between devices, step(): lax.ppermute(gathered, whole, swapped_bit(slabs, cols, 2))  1.87 us
  transfers between devices with their start and end apart: 17, of which 10 were waited for; matrix products, arithmetic and copies ran while one was open for 0% of the time, Pallas kernels for 2%

profile of v2, /device:TPU:8, one launch (start us, length us, event | category | flops | bytes accessed | tf_op | source)
XLA Modules:
  0.0 38.7 jit_solution(16356545093448210588)
XLA Ops:
  0.6 1.0 %collective-permute-start = (f32[8,8,128]{2,1,0:T(8,128)}, f32[8,8,128]{2,1,0:T(8,128)S(1)}, u32[]{:S(2)}, u32[]{:S(2)}) collective-permute-start(f32[8,8,128]{2,1,0:T(8,128)} %refs_0_.3), channel_id=1, source_target_pairs={{0,3},{1,2},{2,1},{3,0},{4,7},{5,6},{6,5},{7,4},{8,11},{9,10},{10,... | collective-permute-start | bytes 98312 | tf_op jit(solution)/shard_map/ppermute | solution.py:677
  1.6 0.8 %collective-permute-start.1 = (f32[1,1,16]{2,1,0:T(1,128)}, f32[1,1,16]{2,1,0:T(1,128)S(1)}, u32[]{:S(2)}, u32[]{:S(2)}) collective-permute-start(f32[1,1,16]{2,1,0:T(1,128)} %refs_1_.2), channel_id=1, source_target_pairs={{0,3},{1,2},{2,1},{3,0},{4,7},{5,6},{6,5},{7,4},{8,11},{9,10},{10,... | collective-permute-start | bytes 200 | tf_op jit(solution)/shard_map/ppermute | solution.py:678
  2.4 0.8 %pack.1 = (f32[9,8,128]{2,1,0:T(8,128)S(1)}, f32[2,8,128]{2,1,0:T(8,128)S(1)}, f32[2,8,128]{2,1,0:T(8,128)S(1)}, f32[2,8,128]{2,1,0:T(8,128)S(1)}, f32[2,8,128]{2,1,0:T(8,128)S(1)}, /*index=5*/f32[2,8,128]{2,1,0:T(8,128)S(1)}) custom-call(f32[8,8,128]{2,1,0:T(8,128)} %refs_0_.3, f32[1,1,16]{2,1,0:T(1,128)} %refs_1_.2, s32[5,1,128]{2,1,0:T(1,128)} %bitcast.8, ...), custom_call_target="tpu_custom_call" | custom-call | tf_op jit(solution)/shard_map/pack/pallas_call | solution.py:655
  3.3 1.5 %collective-permute-done.1.from_metric = f32[1,1,16]{2,1,0:T(1,128)S(1)} collective-permute-done((f32[1,1,16]{2,1,0:T(1,128)}, f32[1,1,16]{2,1,0:T(1,128)S(1)}, u32[]{:S(2)}, u32[]{:S(2)}) %collective-permute-start.1) | collective-permute-done | bytes 96 | tf_op jit(solution)/shard_map/ppermute | solution.py:678
  4.8 0.0 collective-permute-done.from_source
  4.8 1.9 %collective-permute-start.2 = (f32[2,9,8,128]{3,2,1,0:T(8,128)S(1)}, f32[2,9,8,128]{3,2,1,0:T(8,128)S(1)}, u32[]{:S(2)}, u32[]{:S(2)}) collective-permute-start(f32[2,9,8,128]{3,2,1,0:T(8,128)S(1)} %near_pair.1), channel_id=1, source_target_pairs={{0,5},{1,4},{2,7},{3,6},{4,1},{5,0},{6,3},{7,2},{8,13},{9,12},{10,... | collective-permute-start | bytes 221192 | tf_op jit(solution)/shard_map/ppermute | solution.py:687
  6.6 2.0 %collective-permute-done.2 = f32[2,9,8,128]{3,2,1,0:T(8,128)S(1)} collective-permute-done((f32[2,9,8,128]{3,2,1,0:T(8,128)S(1)}, f32[2,9,8,128]{3,2,1,0:T(8,128)S(1)}, u32[]{:S(2)}, u32[]{:S(2)}) %collective-permute-start.2) | collective-permute-done | bytes 73760 | tf_op jit(solution)/shard_map/ppermute | solution.py:687
  8.7 0.0 copy-start.2
  8.7 0.0 copy-start.3
  8.7 0.0 copy-start
  8.7 0.0 copy-start.4
  8.8 0.0 copy-start.1
  8.8 0.7 %collective-permute-start.3 = (f32[26,8,128]{2,1,0:T(8,128)S(1)}, f32[26,8,128]{2,1,0:T(8,128)S(1)}, u32[]{:S(2)}, u32[]{:S(2)}) collective-permute-start(f32[26,8,128]{2,1,0:T(8,128)S(1)} %get-tuple-element.30), channel_id=1, source_target_pairs={{0,9},{1,8},{2,11},{3,10},{4,13},{5,12},{6,15},{7,14},{8,1},{9,0},... | collective-permute-start | bytes 319496 | tf_op jit(solution)/shard_map/ppermute | solution.py:697
  9.5 2.2 %collective-permute-start.4 = (f32[26,8,128]{2,1,0:T(8,128)S(1)}, f32[26,8,128]{2,1,0:T(8,128)S(1)}, u32[]{:S(2)}, u32[]{:S(2)}) collective-permute-start(f32[26,8,128]{2,1,0:T(8,128)S(1)} %get-tuple-element.31), channel_id=1, source_target_pairs={{0,1},{1,0},{2,3},{3,2},{4,5},{5,4},{6,7},{7,6},{8,17},{9,16},{10,... | collective-permute-start | bytes 319496 | tf_op jit(solution)/shard_map/ppermute | solution.py:697
  11.7 0.6 %collective-permute-start.5 = (f32[4,9,8,128]{3,2,1,0:T(8,128)S(1)}, f32[4,9,8,128]{3,2,1,0:T(8,128)S(1)}, u32[]{:S(2)}, u32[]{:S(2)}) collective-permute-start(f32[4,9,8,128]{3,2,1,0:T(8,128)S(1)} %pad_maximum_fusion.gathered.refs_4_), channel_id=1, source_target_pairs={{0,1},{1,0},{2,3},{3,2},{4,5},{5,4},{6,7},{7,6},{8,9},{9,8},{10,11... | collective-permute-start | bytes 442376 | tf_op jit(solution)/shard_map/ppermute | solution.py:704
  12.3 1.0 %collective-permute-done.3.refs_5_ = f32[26,8,128]{2,1,0:T(8,128)S(1)} collective-permute-done((f32[26,8,128]{2,1,0:T(8,128)S(1)}, f32[26,8,128]{2,1,0:T(8,128)S(1)}, u32[]{:S(2)}, u32[]{:S(2)}) %collective-permute-start.3) | collective-permute-done | bytes 106528 | tf_op jit(solution)/shard_map/ppermute | solution.py:697
  13.3 0.9 %collective-permute-start.6 = (f32[26,8,128]{2,1,0:T(8,128)S(1)}, f32[26,8,128]{2,1,0:T(8,128)S(1)}, u32[]{:S(2)}, u32[]{:S(2)}) collective-permute-start(f32[26,8,128]{2,1,0:T(8,128)S(1)} %collective-permute-done.3.refs_5_), channel_id=1, source_target_pairs={{0,1},{1,0},{2,3},{3,2},{4,5},{5,4},{6,7},{7,6},{8,9},{9,8},{10,11... | collective-permute-start | bytes 319496 | tf_op jit(solution)/shard_map/ppermute | solution.py:704
  14.2 0.8 %collective-permute-done.4.refs_6_ = f32[26,8,128]{2,1,0:T(8,128)S(1)} collective-permute-done((f32[26,8,128]{2,1,0:T(8,128)S(1)}, f32[26,8,128]{2,1,0:T(8,128)S(1)}, u32[]{:S(2)}, u32[]{:S(2)}) %collective-permute-start.4) | collective-permute-done | bytes 106528 | tf_op jit(solution)/shard_map/ppermute | solution.py:697
  15.0 0.0 collective-permute-start.7
  15.1 1.9 %collective-permute-start.8 = (f32[2,8,128]{2,1,0:T(8,128)S(1)}, f32[2,8,128]{2,1,0:T(8,128)S(1)}, u32[]{:S(2)}, u32[]{:S(2)}) collective-permute-start(f32[2,8,128]{2,1,0:T(8,128)S(1)} %get-tuple-element.33), channel_id=1, source_target_pairs={{0,2},{1,3},{2,0},{3,1},{4,6},{5,7},{6,4},{7,5},{8,10},{9,11},{10,... | collective-permute-start | bytes 24584 | tf_op jit(solution)/shard_map/ppermute | solution.py:674
  17.0 0.1 collective-permute-start.9
  17.1 1.6 %collective-permute-done.8.refs_2_.refs_12_ = f32[2,8,128]{2,1,0:T(8,128)S(1)} collective-permute-done((f32[2,8,128]{2,1,0:T(8,128)S(1)}, f32[2,8,128]{2,1,0:T(8,128)S(1)}, u32[]{:S(2)}, u32[]{:S(2)}) %collective-permute-start.8) | collective-permute-done | bytes 8224 | tf_op jit(solution)/shard_map/ppermute | solution.py:674
  18.7 1.6 %collective-permute-start.10 = (f32[2,8,128]{2,1,0:T(8,128)S(1)}, f32[2,8,128]{2,1,0:T(8,128)S(1)}, u32[]{:S(2)}, u32[]{:S(2)}) collective-permute-start(f32[2,8,128]{2,1,0:T(8,128)S(1)} %get-tuple-element.35), channel_id=1, source_target_pairs={{0,4},{1,5},{2,6},{3,7},{4,0},{5,1},{6,2},{7,3},{8,12},{9,13},{10,... | collective-permute-start | bytes 24584 | tf_op jit(solution)/shard_map/ppermute | solution.py:674
  20.3 2.2 %collective-permute-done.9.refs_3_.refs_13_ = f32[2,8,128]{2,1,0:T(8,128)S(1)} collective-permute-done((f32[2,8,128]{2,1,0:T(8,128)S(1)}, f32[2,8,128]{2,1,0:T(8,128)S(1)}, u32[]{:S(2)}, u32[]{:S(2)}) %collective-permute-start.9) | collective-permute-done | bytes 8224 | tf_op jit(solution)/shard_map/ppermute | solution.py:674
  22.4 0.0 collective-permute-start.11
  22.4 0.0 collective-permute-done.10.refs_4_.refs_14_
  22.5 4.5 %collective-permute-done.11.refs_5_.refs_15_ = f32[2,8,128]{2,1,0:T(8,128)S(1)} collective-permute-done((f32[2,8,128]{2,1,0:T(8,128)S(1)}, f32[2,8,128]{2,1,0:T(8,128)S(1)}, u32[]{:S(2)}, u32[]{:S(2)}) %collective-permute-start.11) | collective-permute-done | bytes 8224 | tf_op jit(solution)/shard_map/ppermute | solution.py:674
  27.0 0.0 copy-done
  27.0 0.1 bases.1
  27.1 0.0 collective-permute-done.5.refs_7_
  27.1 0.0 collective-permute-done.6.refs_8_
  27.1 0.0 collective-permute-done.7.refs_9_
  27.2 0.0 copy-done.2
  27.2 0.0 copy-done.3
  27.2 0.0 copy-done.4
  27.2 0.0 copy-done.1
  27.2 2.3 %sweeps_and_droplets.1 = (f32[8,8,128]{2,1,0:T(8,128)S(1)}, f32[3,8,8,128]{3,2,1,0:T(8,128)S(1)}, f32[3,8,128]{2,1,0:T(8,128)S(1)}, f32[8,128]{1,0:T(8,128)S(1)}...) custom-call(f32[33,8,128]{2,1,0:T(8,128)S(1)} %copy-done, ...), custom_call_target="tpu_custom_call" | custom-call | tf_op jit(solution)/shard_map/sweeps_and_droplets/pallas_call | solution.py:722
  29.5 0.1 collective-permute-start.12
  29.6 1.2 %collective-permute-done.12.got = f32[12,8,128]{2,1,0:T(8,128)S(1)} collective-permute-done((f32[12,8,128]{2,1,0:T(8,128)S(1)}, f32[12,8,128]{2,1,0:T(8,128)S(1)}, u32[]{:S(2)}, u32[]{:S(2)}) %collective-permute-start.12) | collective-permute-done | bytes 49184 | tf_op jit(solution)/shard_map/ppermute | solution.py:768
  30.9 0.1 collective-permute-start.13
  30.9 1.2 %collective-permute-start.14 = (f32[4,8,128]{2,1,0:T(8,128)S(1)}, f32[4,8,128]{2,1,0:T(8,128)S(1)}, u32[]{:S(2)}, u32[]{:S(2)}) collective-permute-start(f32[4,8,128]{2,1,0:T(8,128)S(1)} %get-tuple-element.48), channel_id=1, source_target_pairs={{0,1},{1,0},{2,5},{3,4},{4,3},{5,2},{6,9},{7,8},{8,7},{9,6},{10,13... | collective-permute-start | bytes 49160 | tf_op jit(solution)/shard_map/ppermute | solution.py:756
  32.1 2.0 %collective-permute-start.15 = (f32[8,128]{1,0:T(8,128)S(1)}, f32[8,128]{1,0:T(8,128)S(1)}, u32[]{:S(2)}, u32[]{:S(2)}) collective-permute-start(f32[8,128]{1,0:T(8,128)S(1)} %get-tuple-element.50), channel_id=1, source_target_pairs={{0,4},{1,5},{2,6},{3,7},{4,0},{5,1},{6,2},{7,3},{8,12},{9,13},{10,... | collective-permute-start | bytes 12296 | tf_op jit(solution)/shard_map/ppermute | solution.py:756
  34.1 0.0 collective-permute-start.16
  34.1 1.6 %collective-permute-done.15.refs_5_ = f32[8,128]{1,0:T(8,128)S(1)} collective-permute-done((f32[8,128]{1,0:T(8,128)S(1)}, f32[8,128]{1,0:T(8,128)S(1)}, u32[]{:S(2)}, u32[]{:S(2)}) %collective-permute-start.15) | collective-permute-done | bytes 4128 | tf_op jit(solution)/shard_map/ppermute | solution.py:756
  35.7 2.3 %collective-permute-done.16.refs_6_ = f32[8,128]{1,0:T(8,128)S(1)} collective-permute-done((f32[8,128]{1,0:T(8,128)S(1)}, f32[8,128]{1,0:T(8,128)S(1)}, u32[]{:S(2)}, u32[]{:S(2)}) %collective-permute-start.16) | collective-permute-done | bytes 4128 | tf_op jit(solution)/shard_map/ppermute | solution.py:756
  38.1 0.0 collective-permute-done.13.refs_2_
  38.1 0.0 collective-permute-done.14.refs_3_
  38.1 0.7 %stream_faces.1 = (f32[8,8,128]{2,1,0:T(8,128)}, f32[3,8,8,128]{3,2,1,0:T(8,128)}, f32[15,1,128]{2,1,0:T(1,128)}) custom-call(f32[8,8,128]{2,1,0:T(8,128)S(1)} %get-tuple-element.40.refs_0_, f32[3,8,8,128]{3,2,1,0:T(8,128)S(1)} %get-tuple-element.46.refs_1_, f32[4,8,128]{2,1,0:T(8,128)S(1)} %collective-permute-done.13.refs_2_, ...), custom_call_target="tpu_custom_call" | custom-call | tf_op jit(solution)/shard_map/stream_faces/pallas_call | solution.py:793
  (5 shorter events, 0.1 us)
Async XLA Ops:
  0.6 4.1 %collective-permute-start = (f32[8,8,128]{2,1,0:T(8,128)}, f32[8,8,128]{2,1,0:T(8,128)S(1)}, u32[]{:S(2)}, u32[]{:S(2)}) collective-permute-start(f32[8,8,128]{2,1,0:T(8,128)} %refs_0_.3), channel_id=1, source_target_pairs={{0,3},{1,2},{2,1},{3,0},{4,7},{5,6},{6,5},{7,4},{8,11},{9,10},{10,... | collective-permute-start | bytes 98312 | tf_op jit(solution)/shard_map/ppermute | solution.py:677
  1.6 3.1 %collective-permute-start.1 = (f32[1,1,16]{2,1,0:T(1,128)}, f32[1,1,16]{2,1,0:T(1,128)S(1)}, u32[]{:S(2)}, u32[]{:S(2)}) collective-permute-start(f32[1,1,16]{2,1,0:T(1,128)} %refs_1_.2), channel_id=1, source_target_pairs={{0,3},{1,2},{2,1},{3,0},{4,7},{5,6},{6,5},{7,4},{8,11},{9,10},{10,... | collective-permute-start | bytes 200 | tf_op jit(solution)/shard_map/ppermute | solution.py:678
  4.8 3.9 %collective-permute-start.2 = (f32[2,9,8,128]{3,2,1,0:T(8,128)S(1)}, f32[2,9,8,128]{3,2,1,0:T(8,128)S(1)}, u32[]{:S(2)}, u32[]{:S(2)}) collective-permute-start(f32[2,9,8,128]{3,2,1,0:T(8,128)S(1)} %near_pair.1), channel_id=1, source_target_pairs={{0,5},{1,4},{2,7},{3,6},{4,1},{5,0},{6,3},{7,2},{8,13},{9,12},{10,... | collective-permute-start | bytes 221192 | tf_op jit(solution)/shard_map/ppermute | solution.py:687
  8.7 18.5 %copy-start.2 = (bf16[256,256]{1,0:T(8,128)(2,1)S(1)}, bf16[256,256]{1,0:T(8,128)(2,1)}, u32[]{:S(2)}) copy-start(bf16[256,256]{1,0:T(8,128)(2,1)} %constant.9.clone.refs_1_) | copy-start | bytes 393220
  8.7 18.5 %copy-start.3 = (f32[3,8,8,128]{3,2,1,0:T(8,128)S(1)}, f32[3,8,8,128]{3,2,1,0:T(8,128)}, u32[]{:S(2)}) copy-start(f32[3,8,8,128]{3,2,1,0:T(8,128)} %refs_10_.1) | copy-start | bytes 294916
  8.7 18.3 %copy-start = (f32[33,8,128]{2,1,0:T(8,128)S(1)}, f32[33,8,128]{2,1,0:T(8,128)}, u32[]{:S(2)}) copy-start(f32[33,8,128]{2,1,0:T(8,128)} %constant.8.clone.refs_0_) | copy-start | bytes 405508
  8.7 18.5 %copy-start.4 = (bf16[256,128]{1,0:T(8,128)(2,1)S(1)}, bf16[256,128]{1,0:T(8,128)(2,1)}, u32[]{:S(2)}) copy-start(bf16[256,128]{1,0:T(8,128)(2,1)} %constant.11.clone.refs_3_) | copy-start | bytes 196612
  8.8 18.4 %copy-start.1 = (bf16[256,256]{1,0:T(8,128)(2,1)S(1)}, bf16[256,256]{1,0:T(8,128)(2,1)}, u32[]{:S(2)}) copy-start(bf16[256,256]{1,0:T(8,128)(2,1)} %constant.10.clone.refs_2_) | copy-start | bytes 393220
  8.8 4.5 %collective-permute-start.3 = (f32[26,8,128]{2,1,0:T(8,128)S(1)}, f32[26,8,128]{2,1,0:T(8,128)S(1)}, u32[]{:S(2)}, u32[]{:S(2)}) collective-permute-start(f32[26,8,128]{2,1,0:T(8,128)S(1)} %get-tuple-element.30), channel_id=1, source_target_pairs={{0,9},{1,8},{2,11},{3,10},{4,13},{5,12},{6,15},{7,14},{8,1},{9,0},... | collective-permute-start | bytes 319496 | tf_op jit(solution)/shard_map/ppermute | solution.py:697
  9.5 5.5 %collective-permute-start.4 = (f32[26,8,128]{2,1,0:T(8,128)S(1)}, f32[26,8,128]{2,1,0:T(8,128)S(1)}, u32[]{:S(2)}, u32[]{:S(2)}) collective-permute-start(f32[26,8,128]{2,1,0:T(8,128)S(1)} %get-tuple-element.31), channel_id=1, source_target_pairs={{0,1},{1,0},{2,3},{3,2},{4,5},{5,4},{6,7},{7,6},{8,17},{9,16},{10,... | collective-permute-start | bytes 319496 | tf_op jit(solution)/shard_map/ppermute | solution.py:697
  11.7 15.4 %collective-permute-start.5 = (f32[4,9,8,128]{3,2,1,0:T(8,128)S(1)}, f32[4,9,8,128]{3,2,1,0:T(8,128)S(1)}, u32[]{:S(2)}, u32[]{:S(2)}) collective-permute-start(f32[4,9,8,128]{3,2,1,0:T(8,128)S(1)} %pad_maximum_fusion.gathered.refs_4_), channel_id=1, source_target_pairs={{0,1},{1,0},{2,3},{3,2},{4,5},{5,4},{6,7},{7,6},{8,9},{9,8},{10,11... | collective-permute-start | bytes 442376 | tf_op jit(solution)/shard_map/ppermute | solution.py:704
  13.3 13.8 %collective-permute-start.6 = (f32[26,8,128]{2,1,0:T(8,128)S(1)}, f32[26,8,128]{2,1,0:T(8,128)S(1)}, u32[]{:S(2)}, u32[]{:S(2)}) collective-permute-start(f32[26,8,128]{2,1,0:T(8,128)S(1)} %collective-permute-done.3.refs_5_), channel_id=1, source_target_pairs={{0,1},{1,0},{2,3},{3,2},{4,5},{5,4},{6,7},{7,6},{8,9},{9,8},{10,11... | collective-permute-start | bytes 319496 | tf_op jit(solution)/shard_map/ppermute | solution.py:704
  15.0 12.1 %collective-permute-start.7 = (f32[26,8,128]{2,1,0:T(8,128)S(1)}, f32[26,8,128]{2,1,0:T(8,128)S(1)}, u32[]{:S(2)}, u32[]{:S(2)}) collective-permute-start(f32[26,8,128]{2,1,0:T(8,128)S(1)} %collective-permute-done.4.refs_6_), channel_id=1, source_target_pairs={{0,1},{1,0},{2,3},{3,2},{4,5},{5,4},{6,7},{7,6},{8,9},{9,8},{10,11... | collective-permute-start | bytes 319496 | tf_op jit(solution)/shard_map/ppermute | solution.py:704
  15.1 3.7 %collective-permute-start.8 = (f32[2,8,128]{2,1,0:T(8,128)S(1)}, f32[2,8,128]{2,1,0:T(8,128)S(1)}, u32[]{:S(2)}, u32[]{:S(2)}) collective-permute-start(f32[2,8,128]{2,1,0:T(8,128)S(1)} %get-tuple-element.33), channel_id=1, source_target_pairs={{0,2},{1,3},{2,0},{3,1},{4,6},{5,7},{6,4},{7,5},{8,10},{9,11},{10,... | collective-permute-start | bytes 24584 | tf_op jit(solution)/shard_map/ppermute | solution.py:674
  17.0 5.5 %collective-permute-start.9 = (f32[2,8,128]{2,1,0:T(8,128)S(1)}, f32[2,8,128]{2,1,0:T(8,128)S(1)}, u32[]{:S(2)}, u32[]{:S(2)}) collective-permute-start(f32[2,8,128]{2,1,0:T(8,128)S(1)} %get-tuple-element.34), channel_id=1, source_target_pairs={{0,1},{1,0},{2,4},{3,5},{4,2},{5,3},{6,8},{7,9},{8,6},{9,7},{10,12... | collective-permute-start | bytes 24584 | tf_op jit(solution)/shard_map/ppermute | solution.py:674
  18.7 3.7 %collective-permute-start.10 = (f32[2,8,128]{2,1,0:T(8,128)S(1)}, f32[2,8,128]{2,1,0:T(8,128)S(1)}, u32[]{:S(2)}, u32[]{:S(2)}) collective-permute-start(f32[2,8,128]{2,1,0:T(8,128)S(1)} %get-tuple-element.35), channel_id=1, source_target_pairs={{0,4},{1,5},{2,6},{3,7},{4,0},{5,1},{6,2},{7,3},{8,12},{9,13},{10,... | collective-permute-start | bytes 24584 | tf_op jit(solution)/shard_map/ppermute | solution.py:674
  22.4 4.5 %collective-permute-start.11 = (f32[2,8,128]{2,1,0:T(8,128)S(1)}, f32[2,8,128]{2,1,0:T(8,128)S(1)}, u32[]{:S(2)}, u32[]{:S(2)}) collective-permute-start(f32[2,8,128]{2,1,0:T(8,128)S(1)} %get-tuple-element.36), channel_id=1, source_target_pairs={{0,1},{1,0},{2,3},{3,2},{4,8},{5,9},{6,10},{7,11},{8,4},{9,5},{10,... | collective-permute-start | bytes 24584 | tf_op jit(solution)/shard_map/ppermute | solution.py:674
  29.5 1.3 %collective-permute-start.12 = (f32[12,8,128]{2,1,0:T(8,128)S(1)}, f32[12,8,128]{2,1,0:T(8,128)S(1)}, u32[]{:S(2)}, u32[]{:S(2)}) collective-permute-start(f32[12,8,128]{2,1,0:T(8,128)S(1)} %bundle.1), channel_id=1, source_target_pairs={{0,1},{1,0},{2,3},{3,2},{4,5},{5,4},{6,7},{7,6},{8,9},{9,8},{10,11... | collective-permute-start | bytes 147464 | tf_op jit(solution)/shard_map/ppermute | solution.py:768
  30.9 7.2 %collective-permute-start.13 = (f32[4,8,128]{2,1,0:T(8,128)S(1)}, f32[4,8,128]{2,1,0:T(8,128)S(1)}, u32[]{:S(2)}, u32[]{:S(2)}) collective-permute-start(f32[4,8,128]{2,1,0:T(8,128)S(1)} %get-tuple-element.47), channel_id=1, source_target_pairs={{0,3},{1,2},{2,1},{3,0},{4,7},{5,6},{6,5},{7,4},{8,11},{9,10},{10,... | collective-permute-start | bytes 49160 | tf_op jit(solution)/shard_map/ppermute | solution.py:756
  30.9 7.1 %collective-permute-start.14 = (f32[4,8,128]{2,1,0:T(8,128)S(1)}, f32[4,8,128]{2,1,0:T(8,128)S(1)}, u32[]{:S(2)}, u32[]{:S(2)}) collective-permute-start(f32[4,8,128]{2,1,0:T(8,128)S(1)} %get-tuple-element.48), channel_id=1, source_target_pairs={{0,1},{1,0},{2,5},{3,4},{4,3},{5,2},{6,9},{7,8},{8,7},{9,6},{10,13... | collective-permute-start | bytes 49160 | tf_op jit(solution)/shard_map/ppermute | solution.py:756
  32.1 3.6 %collective-permute-start.15 = (f32[8,128]{1,0:T(8,128)S(1)}, f32[8,128]{1,0:T(8,128)S(1)}, u32[]{:S(2)}, u32[]{:S(2)}) collective-permute-start(f32[8,128]{1,0:T(8,128)S(1)} %get-tuple-element.50), channel_id=1, source_target_pairs={{0,4},{1,5},{2,6},{3,7},{4,0},{5,1},{6,2},{7,3},{8,12},{9,13},{10,... | collective-permute-start | bytes 12296 | tf_op jit(solution)/shard_map/ppermute | solution.py:756
  34.1 3.9 %collective-permute-start.16 = (f32[8,128]{1,0:T(8,128)S(1)}, f32[8,128]{1,0:T(8,128)S(1)}, u32[]{:S(2)}, u32[]{:S(2)}) collective-permute-start(f32[8,128]{1,0:T(8,128)S(1)} %get-tuple-element.51), channel_id=1, source_target_pairs={{0,1},{1,0},{2,3},{3,2},{4,9},{5,8},{6,11},{7,10},{8,5},{9,4},{10,... | collective-permute-start | bytes 12296 | tf_op jit(solution)/shard_map/ppermute | solution.py:756
